TPU v7x, 32 devices: a whole 2x2x4 slice. The times are simulated.
32 devices in a mesh: segment: 4 (over y, x), vocab: 8 (over z, core).
Axes of the slice: x: 2, y: 2, z: 4, core: 2. Of those that a mesh axis runs over, the one named last changes fastest.
Arguments:
- trunk_out: bfloat16 [160, 7168], P(None, 'vocab'), may hold values from -12 to 12
- embeds: bfloat16 [164, 7168], P(None, 'vocab'), may hold values from -12 to 12
- token_ids: int32 [164], replicated, may hold values from 0 to 8191
- module_weight: bfloat16 [4, 2, 7168, 7168], P('segment', None, 'vocab'), may hold values from -0.046875 to 0.046875
- hidden_gain: bfloat16 [3, 7168], P(None, 'vocab'), may hold values from 0.25 to 1.75
- embed_gain: bfloat16 [3, 7168], P(None, 'vocab'), may hold values from 0.25 to 1.75
- out_gain: bfloat16 [4, 7168], P('segment'), may hold values from 0.25 to 1.75
- head_weight: bfloat16 [7168, 8192], P('segment', 'vocab'), may hold values from -0.21260502 to 0.21260502
Outputs:
- losses: float32 [4, 160], P('segment')
All inputs are finite; a program needn't handle non-finite values.
Results may differ from a plain program's by a relative error of at most 0.00095.
Values may be sent and summed in bfloat16 or wider, within the bound.
No kernel may reach another device: no remote copies, remote signals or barrier semaphores. Data moves between devices by JAX's collectives and lax.ppermute only.
A program may use at most 128 MiB of HBM per device.

v0:
```python
import jax
import jax.numpy as jnp
from jax import lax
from jax.sharding import PartitionSpec as P


EPSILON = 1e-06
CORES = 2
BOTH = ("segment", "vocab")
WIRE = jnp.float16


class Grid:
    def __init__(self):
        self.sections = lax.axis_size("segment")
        self.shards = lax.axis_size("vocab")
        self.chips = self.shards // CORES
        self.section = lax.axis_index("segment")
        self.shard = lax.axis_index("vocab")
        self.chip = self.shard // CORES
        self.core = self.shard % CORES

    def send(self, block, target, sources=None):
        pairs = []
        for s in range(self.sections) if sources is None else sources:
            for z in range(self.chips):
                for c in range(CORES):
                    ts, tz, tc = target(s, z, c)
                    pairs.append((s * self.shards + z * CORES + c, ts * self.shards + tz * CORES + tc))
        return lax.ppermute(block, BOTH, pairs)

    def swap_core(self, block):
        return self.send(block, lambda s, z, c: (s, z, 1 - c))

    def swap_chip(self, block, d):
        return self.send(block, lambda s, z, c: (s, z ^ d, c))

    def swap_section(self, block, d):
        return self.send(block, lambda s, z, c: (s ^ d, z, c))

    def combine(self, value, merge):
        value = merge(value, self.swap_core(value))
        values = [value]
        for d in range(1, self.chips):
            values.append(self.swap_chip(value, d))
        while len(values) > 1:
            values = [merge(a, b) for a, b in zip(values[0::2], values[1::2])]
        return values[0]


def merge_softmax(a, b):
    top = jnp.maximum(a[0], b[0])
    total = a[1] * jnp.exp(a[0] - top) + b[1] * jnp.exp(b[0] - top)
    return jnp.stack([top, total, a[2] + b[2]])


def per_device(
    trunk_out, embeds, token_ids, module_weight, hidden_gain, embed_gain, out_gain, head_weight
):
    grid = Grid()
    sections, chips, section, chip, core = grid.sections, grid.chips, grid.section, grid.chip, grid.core
    tokens, width = trunk_out.shape
    whole_width = module_weight.shape[3]
    vocab_width = head_weight.shape[1]
    depth_count = hidden_gain.shape[0]
    last = depth_count
    group = chips // sections
    part_rows = tokens // sections
    add = lambda a, b: a + b

    def squares(rows):
        return jnp.sum(rows * rows, axis=1)

    def scale_of(total, count=whole_width):
        return lax.rsqrt(total / count + EPSILON)

    def narrow(values):
        return values.astype(jnp.bfloat16)

    def wide(values):
        return values.astype(jnp.float32)

    def pick_index(values, i):
        return lax.dynamic_index_in_dim(values, i, 0, keepdims=False)

    turned = grid.send(trunk_out, lambda a, z, c: (z // group, a * group + z % group, c))
    hidden = wide(trunk_out)
    embed_rows = wide(lax.dynamic_slice_in_dim(embeds, section, tokens, 0))
    first = grid.combine(jnp.stack([squares(hidden), squares(embed_rows)]), add)
    scale = scale_of(first[0])
    first_scale = scale
    embed_scale = scale_of(first[1])
    module_index = jnp.maximum(section - 1, 0)
    own_embed_gain = wide(pick_index(embed_gain, module_index))
    own_hidden_gain = wide(pick_index(hidden_gain, module_index))
    embed_input = narrow(embed_rows * own_embed_gain)
    span = CORES * width

    def columns_of(half, i):
        weights = lax.dynamic_slice(
            module_weight, (0, half, 0, i * span), (1, 1, module_weight.shape[2], span)
        )
        return weights.reshape(module_weight.shape[2], span)

    def product(rows, half, i):
        return jnp.dot(rows, columns_of(half, i), preferred_element_type=jnp.float32)

    def paired_partial(rows, i, embed_product, apart=False):
        partial = product(rows, 0, i)
        if apart:
            partial = lax.optimization_barrier(partial)
        partial = partial * scale[:, None] + embed_product * embed_scale[:, None]
        even, odd = partial[:, :width], partial[:, width:]
        mine = jnp.where(core == 0, even, odd)
        theirs = jnp.where(core == 0, odd, even).astype(WIRE)
        got = grid.swap_core(theirs)
        return (mine + wide(got)).astype(WIRE)

    def gathered_gain():
        parts = [out_gain]
        for d in range(1, sections):
            parts.append(grid.swap_section(out_gain, d))
        return parts

    def gain_slice(k, start, size):
        out = lax.dynamic_slice_in_dim(gains[0], start, size, 1)
        for d in range(1, sections):
            out = jnp.where((section ^ d) == k, lax.dynamic_slice_in_dim(gains[d], start, size, 1), out)
        return wide(out[0])

    section_start = section * (whole_width // sections)
    section_width = whole_width // sections

    def both_halves(mine):
        other = grid.swap_core(mine)
        even = jnp.where(core == 0, mine, other)
        odd = jnp.where(core == 0, other, mine)
        return [half[r] for r in range(group) for half in (even, odd)]

    def head_product(pieces):
        logits = 0.0
        for i, piece in enumerate(pieces):
            piece_logits = jnp.dot(piece, head_weight[i * width : (i + 1) * width], preferred_element_type=jnp.float32)
            logits = logits + piece_logits
        return logits

    def broadcast_column(block, at):
        holders = range(at * group, (at + 1) * group)
        out = [jnp.where(chip == holder, block, jnp.zeros_like(block)) for holder in holders]
        for d in range(1, chips):
            pairs = [
                (s * grid.shards + z * CORES + c, s * grid.shards + (z ^ d) * CORES + c)
                for s in range(sections)
                for z in holders
                for c in range(CORES)
            ]
            got = lax.ppermute(block, BOTH, pairs)
            for r, holder in enumerate(holders):
                out[r] = jnp.where((chip ^ d) == holder, got, out[r])
        return jnp.stack(out)

    partial_logits = []
    gains = None
    order = [d for pair in zip(reversed(range(chips)), range(chips)) for d in pair][:chips]
    embed_products = {}
    for k in range(1, depth_count):
        received = []
        rows = narrow(hidden * own_hidden_gain)
        for n, d in enumerate(order):
            if k == 1:
                embed_products[d] = lax.optimization_barrier(product(embed_input, 1, chip ^ d))
            paired = paired_partial(rows, chip ^ d, embed_products[d], k > 1 and n == 0)
            received.append(
                grid.send(paired, lambda s, z, c: ((s + 1) % sections, z ^ d, c), sources=(k,))
            )
        if k == 1:
            gains = gathered_gain()
            if group == 1:
                spread = turned[None]
            else:
                spread = jnp.zeros((group, tokens, width), trunk_out.dtype)
                for e in range(group):
                    swapped = turned if e == 0 else grid.swap_chip(turned, e)
                    spread = lax.dynamic_update_index_in_dim(spread, swapped, (chip ^ e) % group, 0)
            pieces = both_halves(spread)
            columns = gain_slice(0, section_start, section_width)
            pieces = [
                narrow(wide(piece) * first_scale[:, None] * columns[i * width : (i + 1) * width])
                for i, piece in enumerate(pieces)
            ]
            partial_logits.append(head_product(pieces))
        total = wide(narrow(sum(wide(part) for part in received)))
        arrived = section == k + 1
        hidden = jnp.where(arrived, total, hidden)
        scale = jnp.where(arrived, scale_of(grid.combine(squares(hidden)[None], add)[0]), scale)
        apart, apart_scale = lax.optimization_barrier((hidden, scale))
        rows = narrow(apart * apart_scale[:, None] * gain_slice(k, grid.shard * width, width))
        at = sections // 2
        hopped = grid.send(
            rows, lambda a, z, c: (z // group, at * group + z % group, c), sources=(k + 1,)
        )
        partial_logits.append(head_product(both_halves(broadcast_column(hopped, at))))

    rows = narrow(hidden * own_hidden_gain)
    part = jnp.zeros((group, tokens, width), WIRE)
    for n, e in enumerate(reversed(range(sections))):
        s = last ^ e
        blocks = []
        for r in range(group):
            i = s * group + r
            embed_product = embed_products[0]
            for d in range(1, chips):
                embed_product = jnp.where((chip ^ d) == i, embed_products[d], embed_product)
            blocks.append(paired_partial(rows, i, embed_product, n + r == 0))
        block = jnp.stack(blocks)
        if s != last:
            block = grid.send(block, lambda a, z, c: (s, z, c), sources=(last,))
        part = jnp.where(section == s, block, part)
    chip_rows = tokens // chips
    part = part.reshape(group, chips, chip_rows, width).transpose(1, 0, 2, 3)
    total = wide(pick_index(part, chip))
    for d in reversed(range(1, chips)):
        got = grid.swap_chip(pick_index(part, chip ^ d), d)
        total = total + wide(got)
    mine = narrow(total)
    spread = jnp.zeros((chips, group, chip_rows, width), jnp.bfloat16)
    spread = lax.dynamic_update_index_in_dim(spread, mine, chip, 0)
    for d in reversed(range(1, chips)):
        got = grid.swap_chip(mine, d)
        spread = lax.dynamic_update_index_in_dim(spread, got, chip ^ d, 0)
    spread = spread.transpose(1, 0, 2, 3).reshape(group, tokens, width)
    pieces = [wide(piece) for piece in both_halves(spread)]
    last_squares = sum(squares(piece) for piece in pieces)
    last_scale = scale_of(last_squares, section_width)
    columns = gain_slice(last, section_start, section_width)
    logits = head_product([narrow(piece * columns[i * width : (i + 1) * width]) for i, piece in enumerate(pieces)])

    def row_part(values, i):
        return lax.dynamic_slice_in_dim(values, i * part_rows, part_rows, 0)

    sent = (logits * last_scale[:, None]).astype(WIRE)
    own_logits = row_part(logits, section)
    square_sum = row_part(last_squares, section)
    gots = []
    for d in reversed(range(1, sections)):
        got_squares = grid.swap_section(row_part(last_squares, section ^ d), d)
        got = grid.swap_section(row_part(sent, section ^ d), d)
        gots.append((got, got_squares))
    for got, got_squares in gots:
        own_logits = own_logits + wide(got) / scale_of(got_squares, section_width)[:, None]
        square_sum = square_sum + got_squares
    own_logits = own_logits * scale_of(square_sum)[:, None]

    early = jnp.stack(partial_logits + [jnp.zeros_like(partial_logits[0])] * (sections - len(partial_logits)))
    sent = early.astype(WIRE)
    rows = pick_index(early, section)
    for d in reversed(range(1, sections)):
        got = grid.swap_section(pick_index(sent, section ^ d), d)
        rows = rows + wide(got)

    def statistics(values, targets):
        column_ids = lax.broadcasted_iota(jnp.int32, values.shape, 1)
        pick = jnp.sum(jnp.where(column_ids == targets[:, None], values, 0.0), axis=1)
        top = jnp.max(values, axis=1)
        total = jnp.sum(jnp.exp(values - top[:, None]), axis=1)
        return jnp.stack([top, total, pick])

    local_ids = token_ids - grid.shard * vocab_width
    early_statistics = statistics(rows, lax.dynamic_slice_in_dim(local_ids, section + 1, tokens, 0))
    late = statistics(
        own_logits, lax.dynamic_slice_in_dim(local_ids, last + 1 + section * part_rows, part_rows, 0)
    )
    late_parts = [
        jnp.where(section == s, late, grid.send(late, lambda a, z, c: (last, z, c), sources=(s,)))
        if s != last
        else late
        for s in range(sections)
    ]
    values = jnp.where(section == last, jnp.concatenate(late_parts, axis=1), early_statistics)
    top, total, pick = grid.combine(values, merge_softmax)
    return (top + jnp.log(total) - pick)[None, :]


def solution(mesh):
    in_specs = (
        P(None, "vocab"),
        P(None, "vocab"),
        P(),
        P("segment", None, "vocab", None),
        P(None, "vocab"),
        P(None, "vocab"),
        P("segment", None),
        P("segment", "vocab"),
    )
    out_specs = P("segment", None)
    return jax.shard_map(per_device, mesh=mesh, in_specs=in_specs, out_specs=out_specs, check_vma=False)
```

profile of v0, /device:TPU:5, one launch (start us, length us, event | category | flops | bytes accessed | tf_op | source)
XLA Modules:
  0.0 270.3 jit_solution(6376805174792265215)
XLA Ops:
  6.7 2.8 %fusion.8 = f32[160,1792]{1,0:T(8,128)S(1)} fusion(bf16[1,2,896,7168]{3,2,1,0:T(8,128)(2,1)} %param.11, s32[]{:T(128)S(6)} %select_n.557, f32[896]{0:T(1024)S(1)} %get-tuple-element.68, bf16[164,896]{1,0:T(8,128)(2,1)} %param.9, s32[]{:T(128)S(6)} %select_n.548), kind=kOutput, calls=%fused_computation.8 | convolution fusion | flops 514232320 | bytes 4648456 | tf_op jit(solution)/shard_map/dot_general | solution.py:106
  9.5 3.8 %fusion.14 = f32[160,1792]{1,0:T(8,128)} fusion(bf16[1,2,896,7168]{3,2,1,0:T(8,128)(2,1)} %param.11, s32[]{:T(128)S(6)} %select_n.554, f32[896]{0:T(1024)S(1)} %get-tuple-element.68, bf16[164,896]{1,0:T(8,128)(2,1)S(1)} %copy-done.4, s32[]{:T(128)S(6)} %select_n.548), kind=kOutput, calls=%fused_computation.14 | convolution fusion | flops 514232320 | bytes 4648968 | tf_op jit(solution)/shard_map/dot_general | solution.py:106
  13.3 3.7 %fusion.20 = f32[160,1792]{1,0:T(8,128)} fusion(bf16[1,2,896,7168]{3,2,1,0:T(8,128)(2,1)} %param.11, s32[]{:T(128)S(6)} %select_n.551, f32[896]{0:T(1024)S(1)} %get-tuple-element.68, bf16[164,896]{1,0:T(8,128)(2,1)S(1)} %copy-done.4, s32[]{:T(128)S(6)} %select_n.548), kind=kOutput, calls=%fused_computation.20 | convolution fusion | flops 514232320 | bytes 4648968 | tf_op jit(solution)/shard_map/dot_general | solution.py:106
  17.0 2.8 %fusion.26 = f32[160,1792]{1,0:T(8,128)S(1)} fusion(bf16[1,2,896,7168]{3,2,1,0:T(8,128)(2,1)} %param.11, s32[]{:T(128)S(6)} %select_n.547, f32[896]{0:T(1024)S(1)} %get-tuple-element.68, bf16[164,896]{1,0:T(8,128)(2,1)S(1)} %copy-done.4, s32[]{:T(128)S(6)} %select_n.548), kind=kOutput, calls=%fused_computation.26 | convolution fusion | flops 514232320 | bytes 4648968 | tf_op jit(solution)/shard_map/dot_general | solution.py:106
  19.9 2.4 collective-permute-start.2
  24.0 2.5 collective-permute-done.3
  26.6 2.8 %fusion.81 = f32[160,1792]{1,0:T(8,128)S(1)} fusion(bf16[1,2,896,7168]{3,2,1,0:T(8,128)(2,1)} %param.11, s32[]{:T(128)S(6)} %select_n.557, f32[160,1792]{1,0:T(8,128)S(1)} %fusion.8, f32[160]{0:T(256)S(1)} %bitcast.226, f32[160]{0:T(256)S(1)} %bitcast.238, bf16[160,896]{1,0:T(8,128)(2,1)S(1)} %copy-done.3, f32[896]{0:T(1024)S(1)} %get-tuple-element.67), kind=kOutput, calls=%fused_computation.60 | convolution fusion | flops 515092480 | bytes 5796612 | tf_op jit(solution)/shard_map/dot_general | solution.py:106
  29.5 1.6 collective-permute-start.10
  31.2 2.7 %fusion.69 = f32[160,1792]{1,0:T(8,128)S(1)} fusion(bf16[1,2,896,7168]{3,2,1,0:T(8,128)(2,1)} %param.11, s32[]{:T(128)S(6)} %select_n.554, f32[160,1792]{1,0:T(8,128)S(1)} %copy-done, f32[160]{0:T(256)S(1)} %bitcast.227, f32[160]{0:T(256)S(1)} %bitcast.239, bf16[160,896]{1,0:T(8,128)(2,1)S(1)} %copy-done.3, f32[896]{0:T(1024)S(1)} %get-tuple-element.67), kind=kOutput, calls=%fused_computation.56 | convolution fusion | flops 515092480 | bytes 5796612 | tf_op jit(solution)/shard_map/dot_general | solution.py:106
  34.0 1.4 collective-permute-start.8
  35.4 2.8 %fusion.57 = f32[160,1792]{1,0:T(8,128)S(1)} fusion(bf16[1,2,896,7168]{3,2,1,0:T(8,128)(2,1)} %param.11, s32[]{:T(128)S(6)} %select_n.551, f32[160,1792]{1,0:T(8,128)S(1)} %copy-done.1, f32[160]{0:T(256)S(1)} %bitcast.228, f32[160]{0:T(256)S(1)} %bitcast.240, bf16[160,896]{1,0:T(8,128)(2,1)S(1)} %copy-done.3, f32[896]{0:T(1024)S(1)} %get-tuple-element.67), kind=kOutput, calls=%fused_computation.52 | convolution fusion | flops 515092480 | bytes 5796612 | tf_op jit(solution)/shard_map/dot_general | solution.py:106
  38.2 2.7 fusion.51
  41.0 1.5 collective-permute-start.6
  43.7 2.9 %collective-permute-start.54 = (bf16[160,896]{1,0:T(8,128)(2,1)S(1)}, bf16[160,896]{1,0:T(8,128)(2,1)S(1)}, u32[]{:S(2)}, u32[]{:S(2)}) collective-permute-start(bf16[160,896]{1,0:T(8,128)(2,1)S(1)} %copy-done.3), channel_id=1, source_target_pairs={{0,0},{1,1},{2,8},{3,9},{4,16},{5,17},{6,24},{7,25},{8,2},{9,3},{1... | collective-permute-start | bytes 860168 | tf_op jit(solution)/shard_map/ppermute | solution.py:30
  50.8 1.5 collective-permute-start.5
  52.4 12.8 %collective-permute-done.54 = bf16[160,896]{1,0:T(8,128)(2,1)S(1)} collective-permute-done((bf16[160,896]{1,0:T(8,128)(2,1)S(1)}, bf16[160,896]{1,0:T(8,128)(2,1)S(1)}, u32[]{:S(2)}, u32[]{:S(2)}) %collective-permute-start.54) | collective-permute-done | bytes 286752 | tf_op jit(solution)/shard_map/ppermute | solution.py:30
  65.2 2.2 collective-permute-start.55
  67.5 17.8 %collective-permute-done.9 = f16[160,896]{1,0:T(8,128)(2,1)S(1)} collective-permute-done((f16[160,896]{1,0:T(8,128)(2,1)S(1)}, f16[160,896]{1,0:T(8,128)(2,1)S(1)}, u32[]{:S(2)}, u32[]{:S(2)}) %collective-permute-start.9) | collective-permute-done | bytes 286752 | tf_op jit(solution)/shard_map/ppermute | solution.py:30
  87.0 8.4 %collective-permute-start.15 = (f32[1,160]{1,0:T(1,128)S(1)}, f32[1,160]{1,0:T(1,128)S(1)}, u32[]{:S(2)}, u32[]{:S(2)}) collective-permute-start(f32[1,160]{1,0:T(1,128)S(1)} %add.415), channel_id=1, source_target_pairs={{0,6},{1,7},{2,4},{3,5},{4,2},{5,3},{6,0},{7,1},{8,14},{9,15},{10,... | collective-permute-start | bytes 1928 | tf_op jit(solution)/shard_map/ppermute | solution.py:30
  95.5 2.7 fusion.28
  98.2 2.7 %fusion.87 = f32[160,1792]{1,0:T(8,128)S(1)} fusion(bf16[160,896]{1,0:T(8,128)(2,1)S(1)} %multiply_convert_fusion.4, bf16[1,2,896,7168]{3,2,1,0:T(8,128)(2,1)} %param.11, s32[]{:T(128)S(6)} %select_n.557, f32[160,1792]{1,0:T(8,128)S(1)} %fusion.8, f32[160]{0:T(256)S(1)} %broadcast_select_fusion.19, f32[160]{0:T(256)S(1)} %bitcast.230), kind=kOutput, calls=%fused_computation.62 | convolution fusion | flops 514662400 | bytes 5793028 | tf_op jit(solution)/shard_map/dot_general | solution.py:106
  102.8 1.8 collective-permute-start.22
  105.9 1.3 collective-permute-start.56
  107.3 1.3 collective-permute-start.23
  108.7 1.6 collective-permute-start.21
  110.4 1.3 collective-permute-start.19
  115.1 7.7 %collective-permute-done.23 = f16[160,896]{1,0:T(8,128)(2,1)S(1)} collective-permute-done((f16[160,896]{1,0:T(8,128)(2,1)S(1)}, f16[160,896]{1,0:T(8,128)(2,1)S(1)}, u32[]{:S(2)}, u32[]{:S(2)}) %collective-permute-start.23) | collective-permute-done | bytes 286752 | tf_op jit(solution)/shard_map/ppermute | solution.py:30
  124.1 6.3 %collective-permute-done.21 = f16[160,896]{1,0:T(8,128)(2,1)S(1)} collective-permute-done((f16[160,896]{1,0:T(8,128)(2,1)S(1)}, f16[160,896]{1,0:T(8,128)(2,1)S(1)}, u32[]{:S(2)}, u32[]{:S(2)}) %collective-permute-start.21) | collective-permute-done | bytes 286752 | tf_op jit(solution)/shard_map/ppermute | solution.py:30
  130.4 6.1 %collective-permute-done.17 = f16[160,896]{1,0:T(8,128)(2,1)S(1)} collective-permute-done((f16[160,896]{1,0:T(8,128)(2,1)S(1)}, f16[160,896]{1,0:T(8,128)(2,1)S(1)}, u32[]{:S(2)}, u32[]{:S(2)}) %collective-permute-start.17) | collective-permute-done | bytes 286752 | tf_op jit(solution)/shard_map/ppermute | solution.py:30
  138.8 6.9 %collective-permute-start.26 = (f32[1,160]{1,0:T(1,128)S(1)}, f32[1,160]{1,0:T(1,128)S(1)}, u32[]{:S(2)}, u32[]{:S(2)}) collective-permute-start(f32[1,160]{1,0:T(1,128)S(1)} %add.431), channel_id=1, source_target_pairs={{0,4},{1,5},{2,6},{3,7},{4,0},{5,1},{6,2},{7,3},{8,12},{9,13},{10,... | collective-permute-start | bytes 1928 | tf_op jit(solution)/shard_map/ppermute | solution.py:30
  145.7 9.2 %collective-permute-start.27 = (f32[1,160]{1,0:T(1,128)S(1)}, f32[1,160]{1,0:T(1,128)S(1)}, u32[]{:S(2)}, u32[]{:S(2)}) collective-permute-start(f32[1,160]{1,0:T(1,128)S(1)} %add.431), channel_id=1, source_target_pairs={{0,6},{1,7},{2,4},{3,5},{4,2},{5,3},{6,0},{7,1},{8,14},{9,15},{10,... | collective-permute-start | bytes 1928 | tf_op jit(solution)/shard_map/ppermute | solution.py:30
  159.6 2.1 collective-permute-start.29
  169.5 6.3 %collective-permute-done.30 = f16[1,160,896]{2,1,0:T(8,128)(2,1)S(1)} collective-permute-done((f16[1,160,896]{2,1,0:T(8,128)(2,1)S(1)}, f16[1,160,896]{2,1,0:T(8,128)(2,1)S(1)}, u32[]{:S(2)}, u32[]{:S(2)}) %collective-permute-start.30) | collective-permute-done | bytes 286752 | tf_op jit(solution)/shard_map/ppermute | solution.py:30
  179.4 20.3 %collective-permute-start.36 = (f16[1,40,896]{2,1,0:T(8,128)(2,1)S(1)}, f16[1,40,896]{2,1,0:T(8,128)(2,1)S(1)}, u32[]{:S(2)}, u32[]{:S(2)}) collective-permute-start(f16[1,40,896]{2,1,0:T(8,128)(2,1)S(1)} %get-tuple-element.49), channel_id=1, source_target_pairs={{0,4},{1,5},{2,6},{3,7},{4,0},{5,1},{6,2},{7,3},{8,12},{9,13},{10,... | collective-permute-start | bytes 215048 | tf_op jit(solution)/shard_map/ppermute | solution.py:30
  200.3 12.2 %collective-permute-done.36 = f16[1,40,896]{2,1,0:T(8,128)(2,1)S(1)} collective-permute-done((f16[1,40,896]{2,1,0:T(8,128)(2,1)S(1)}, f16[1,40,896]{2,1,0:T(8,128)(2,1)S(1)}, u32[]{:S(2)}, u32[]{:S(2)}) %collective-permute-start.36) | collective-permute-done | bytes 71712 | tf_op jit(solution)/shard_map/ppermute | solution.py:30
  212.8 2.4 collective-permute-start.65
  215.1 2.5 collective-permute-start.39
  217.6 1.3 collective-permute-start.40
  218.9 3.1 %collective-permute-done.39 = bf16[1,40,896]{2,1,0:T(8,128)(2,1)S(1)} collective-permute-done((bf16[1,40,896]{2,1,0:T(8,128)(2,1)S(1)}, bf16[1,40,896]{2,1,0:T(8,128)(2,1)S(1)}, u32[]{:S(2)}, u32[]{:S(2)}) %collective-permute-start.39) | collective-permute-done | bytes 71712 | tf_op jit(solution)/shard_map/ppermute | solution.py:30
  222.2 1.7 collective-permute-start.41
  227.0 2.6 collective-permute-start.46
  231.2 3.1 %collective-permute-done.46 = f32[40]{0:T(128)S(1)} collective-permute-done((f32[40]{0:T(128)S(1)}, f32[40]{0:T(128)S(1)}, u32[]{:S(2)}, u32[]{:S(2)}) %collective-permute-start.46) | collective-permute-done | bytes 192 | tf_op jit(solution)/shard_map/ppermute | solution.py:30
  238.3 1.9 collective-permute-start.66
  240.2 1.9 collective-permute-done.45
  244.0 6.7 %collective-permute-start.53 = (f32[3,40]{1,0:T(4,128)S(1)}, f32[3,40]{1,0:T(4,128)S(1)}, u32[]{:S(2)}, u32[]{:S(2)}) collective-permute-start(f32[3,40]{1,0:T(4,128)S(1)} %pad_maximum_fusion.2), channel_id=1, source_target_pairs={{16,24},{17,25},{18,26},{19,27},{20,28},{21,29},{22,30},{23,31}} | collective-permute-start | bytes 1448 | tf_op jit(solution)/shard_map/ppermute | solution.py:30
  253.1 10.3 %collective-permute-start.69 = (f32[3,160]{1,0:T(4,128)S(1)}, f32[3,160]{1,0:T(4,128)S(1)}, u32[]{:S(2)}, u32[]{:S(2)}) collective-permute-start(f32[3,160]{1,0:T(4,128)S(1)} %maximum_select_fusion), channel_id=1, source_target_pairs={{0,1},{1,0},{2,3},{3,2},{4,5},{5,4},{6,7},{7,6},{8,9},{9,8},{10,11... | collective-permute-start | bytes 5768 | tf_op jit(solution)/shard_map/ppermute | solution.py:30
  264.3 1.8 collective-permute-start.72
  266.1 1.8 collective-permute-start.70
  (229 shorter events, 58.8 us)
Async XLA Ops:
  0.0 48.2 %collective-permute-start.42 = (bf16[1,7168]{1,0:T(2,128)(2,1)}, bf16[1,7168]{1,0:T(2,128)(2,1)S(1)}, u32[]{:S(2)}, u32[]{:S(2)}) collective-permute-start(bf16[1,7168]{1,0:T(2,128)(2,1)} %param.14), channel_id=1, source_target_pairs={{0,24},{1,25},{2,26},{3,27},{4,28},{5,29},{6,30},{7,31},{8,16},{9,... | collective-permute-start | bytes 43016 | tf_op jit(solution)/shard_map/ppermute | solution.py:30
  1.2 48.3 %collective-permute-start.43 = (bf16[1,7168]{1,0:T(2,128)(2,1)}, bf16[1,7168]{1,0:T(2,128)(2,1)S(1)}, u32[]{:S(2)}, u32[]{:S(2)}) collective-permute-start(bf16[1,7168]{1,0:T(2,128)(2,1)} %param.14), channel_id=1, source_target_pairs={{0,16},{1,17},{2,18},{3,19},{4,20},{5,21},{6,22},{7,23},{8,24},{9,... | collective-permute-start | bytes 43016 | tf_op jit(solution)/shard_map/ppermute | solution.py:30
  4.6 15.2 %collective-permute-start = (f32[2,160]{1,0:T(2,128)S(1)}, f32[2,160]{1,0:T(2,128)S(1)}, u32[]{:S(2)}, u32[]{:S(2)}) collective-permute-start(f32[2,160]{1,0:T(2,128)S(1)} %pad_maximum_fusion.1), channel_id=1, source_target_pairs={{0,1},{1,0},{2,3},{3,2},{4,5},{5,4},{6,7},{7,6},{8,9},{9,8},{10,11... | collective-permute-start | bytes 3848 | tf_op jit(solution)/shard_map/ppermute | solution.py:30
  23.7 27.1 %collective-permute-start.44 = (bf16[1,7168]{1,0:T(2,128)(2,1)S(1)}, bf16[1,7168]{1,0:T(2,128)(2,1)S(1)}, u32[]{:S(2)}, u32[]{:S(2)}) collective-permute-start(bf16[1,7168]{1,0:T(2,128)(2,1)S(1)} %copy-done.5), channel_id=1, source_target_pairs={{0,8},{1,9},{2,10},{3,11},{4,12},{5,13},{6,14},{7,15},{8,0},{9,1},... | collective-permute-start | bytes 43016 | tf_op jit(solution)/shard_map/ppermute | solution.py:30
  29.5 11.5 %collective-permute-start.10 = (f16[160,896]{1,0:T(8,128)(2,1)S(1)}, f16[160,896]{1,0:T(8,128)(2,1)S(1)}, u32[]{:S(2)}, u32[]{:S(2)}) collective-permute-start(f16[160,896]{1,0:T(8,128)(2,1)S(1)} %select_convert_fusion.8), channel_id=1, source_target_pairs={{0,1},{1,0},{2,3},{3,2},{4,5},{5,4},{6,7},{7,6},{8,9},{9,8},{10,11... | collective-permute-start | bytes 860168 | tf_op jit(solution)/shard_map/ppermute | solution.py:30
  34.0 8.6 %collective-permute-start.8 = (f16[160,896]{1,0:T(8,128)(2,1)S(1)}, f16[160,896]{1,0:T(8,128)(2,1)S(1)}, u32[]{:S(2)}, u32[]{:S(2)}) collective-permute-start(f16[160,896]{1,0:T(8,128)(2,1)S(1)} %select_convert_fusion.9), channel_id=1, source_target_pairs={{0,1},{1,0},{2,3},{3,2},{4,5},{5,4},{6,7},{7,6},{8,9},{9,8},{10,11... | collective-permute-start | bytes 860168 | tf_op jit(solution)/shard_map/ppermute | solution.py:30
  43.7 21.6 %collective-permute-start.54 = (bf16[160,896]{1,0:T(8,128)(2,1)S(1)}, bf16[160,896]{1,0:T(8,128)(2,1)S(1)}, u32[]{:S(2)}, u32[]{:S(2)}) collective-permute-start(bf16[160,896]{1,0:T(8,128)(2,1)S(1)} %copy-done.3), channel_id=1, source_target_pairs={{0,0},{1,1},{2,8},{3,9},{4,16},{5,17},{6,24},{7,25},{8,2},{9,3},{1... | collective-permute-start | bytes 860168 | tf_op jit(solution)/shard_map/ppermute | solution.py:30
  46.7 20.7 %collective-permute-start.11 = (f16[160,896]{1,0:T(8,128)(2,1)S(1)}, f16[160,896]{1,0:T(8,128)(2,1)S(1)}, u32[]{:S(2)}, u32[]{:S(2)}) collective-permute-start(f16[160,896]{1,0:T(8,128)(2,1)S(1)} %add_convert_fusion.10), channel_id=1, source_target_pairs={{8,18},{9,19},{10,16},{11,17},{12,22},{13,23},{14,20},{15,21}} | collective-permute-start | bytes 860168 | tf_op jit(solution)/shard_map/ppermute | solution.py:30
  48.2 37.1 %collective-permute-start.9 = (f16[160,896]{1,0:T(8,128)(2,1)S(1)}, f16[160,896]{1,0:T(8,128)(2,1)S(1)}, u32[]{:S(2)}, u32[]{:S(2)}) collective-permute-start(f16[160,896]{1,0:T(8,128)(2,1)S(1)} %add_convert_fusion.11), channel_id=1, source_target_pairs={{8,20},{9,21},{10,22},{11,23},{12,16},{13,17},{14,18},{15,19}} | collective-permute-start | bytes 860168 | tf_op jit(solution)/shard_map/ppermute | solution.py:30
  49.5 35.8 %collective-permute-start.7 = (f16[160,896]{1,0:T(8,128)(2,1)S(1)}, f16[160,896]{1,0:T(8,128)(2,1)S(1)}, u32[]{:S(2)}, u32[]{:S(2)}) collective-permute-start(f16[160,896]{1,0:T(8,128)(2,1)S(1)} %add_convert_fusion.12), channel_id=1, source_target_pairs={{8,16},{9,17},{10,18},{11,19},{12,20},{13,21},{14,22},{15,23}} | collective-permute-start | bytes 860168 | tf_op jit(solution)/shard_map/ppermute | solution.py:30
  50.8 34.5 %collective-permute-start.5 = (f16[160,896]{1,0:T(8,128)(2,1)S(1)}, f16[160,896]{1,0:T(8,128)(2,1)S(1)}, u32[]{:S(2)}, u32[]{:S(2)}) collective-permute-start(f16[160,896]{1,0:T(8,128)(2,1)S(1)} %add_convert_fusion.13), channel_id=1, source_target_pairs={{8,22},{9,23},{10,20},{11,21},{12,18},{13,19},{14,16},{15,17}} | collective-permute-start | bytes 860168 | tf_op jit(solution)/shard_map/ppermute | solution.py:30
  65.2 46.6 %collective-permute-start.55 = (bf16[1,160,896]{2,1,0:T(8,128)(2,1)S(1)}, bf16[1,160,896]{2,1,0:T(8,128)(2,1)S(1)}, u32[]{:S(2)}, u32[]{:S(2)}) collective-permute-start(bf16[1,160,896]{2,1,0:T(8,128)(2,1)S(1)} %bitcast.225), channel_id=1, source_target_pairs={{0,1},{1,0},{2,3},{3,2},{4,5},{5,4},{6,7},{7,6},{8,9},{9,8},{10,11... | collective-permute-start | bytes 860168 | tf_op jit(solution)/shard_map/ppermute | solution.py:30
  87.0 11.1 %collective-permute-start.14 = (f32[1,160]{1,0:T(1,128)S(1)}, f32[1,160]{1,0:T(1,128)S(1)}, u32[]{:S(2)}, u32[]{:S(2)}) collective-permute-start(f32[1,160]{1,0:T(1,128)S(1)} %add.415), channel_id=1, source_target_pairs={{0,4},{1,5},{2,6},{3,7},{4,0},{5,1},{6,2},{7,3},{8,12},{9,13},{10,... | collective-permute-start | bytes 1928 | tf_op jit(solution)/shard_map/ppermute | solution.py:30
  87.0 11.1 %collective-permute-start.15 = (f32[1,160]{1,0:T(1,128)S(1)}, f32[1,160]{1,0:T(1,128)S(1)}, u32[]{:S(2)}, u32[]{:S(2)}) collective-permute-start(f32[1,160]{1,0:T(1,128)S(1)} %add.415), channel_id=1, source_target_pairs={{0,6},{1,7},{2,4},{3,5},{4,2},{5,3},{6,0},{7,1},{8,14},{9,15},{10,... | collective-permute-start | bytes 1928 | tf_op jit(solution)/shard_map/ppermute | solution.py:30
  105.9 8.5 %collective-permute-start.56 = (bf16[160,896]{1,0:T(8,128)(2,1)S(1)}, bf16[160,896]{1,0:T(8,128)(2,1)S(1)}, u32[]{:S(2)}, u32[]{:S(2)}) collective-permute-start(bf16[160,896]{1,0:T(8,128)(2,1)S(1)} %multiply_convert_fusion.2), channel_id=1, source_target_pairs={{16,4},{17,5},{18,12},{19,13},{20,20},{21,21},{22,28},{23,29}} | collective-permute-start | bytes 860168 | tf_op jit(solution)/shard_map/ppermute | solution.py:30
  107.3 15.5 %collective-permute-start.23 = (f16[160,896]{1,0:T(8,128)(2,1)S(1)}, f16[160,896]{1,0:T(8,128)(2,1)S(1)}, u32[]{:S(2)}, u32[]{:S(2)}) collective-permute-start(f16[160,896]{1,0:T(8,128)(2,1)S(1)} %add_convert_fusion.5), channel_id=1, source_target_pairs={{16,26},{17,27},{18,24},{19,25},{20,30},{21,31},{22,28},{23,29}} | collective-permute-start | bytes 860168 | tf_op jit(solution)/shard_map/ppermute | solution.py:30
  108.7 21.7 %collective-permute-start.21 = (f16[160,896]{1,0:T(8,128)(2,1)S(1)}, f16[160,896]{1,0:T(8,128)(2,1)S(1)}, u32[]{:S(2)}, u32[]{:S(2)}) collective-permute-start(f16[160,896]{1,0:T(8,128)(2,1)S(1)} %add_convert_fusion.6), channel_id=1, source_target_pairs={{16,28},{17,29},{18,30},{19,31},{20,24},{21,25},{22,26},{23,27}} | collective-permute-start | bytes 860168 | tf_op jit(solution)/shard_map/ppermute | solution.py:30
  110.4 20.0 %collective-permute-start.19 = (f16[160,896]{1,0:T(8,128)(2,1)S(1)}, f16[160,896]{1,0:T(8,128)(2,1)S(1)}, u32[]{:S(2)}, u32[]{:S(2)}) collective-permute-start(f16[160,896]{1,0:T(8,128)(2,1)S(1)} %add_convert_fusion.7), channel_id=1, source_target_pairs={{16,24},{17,25},{18,26},{19,27},{20,28},{21,29},{22,30},{23,31}} | collective-permute-start | bytes 860168 | tf_op jit(solution)/shard_map/ppermute | solution.py:30
  111.9 24.7 %collective-permute-start.17 = (f16[160,896]{1,0:T(8,128)(2,1)S(1)}, f16[160,896]{1,0:T(8,128)(2,1)S(1)}, u32[]{:S(2)}, u32[]{:S(2)}) collective-permute-start(f16[160,896]{1,0:T(8,128)(2,1)S(1)} %add_convert_fusion.8), channel_id=1, source_target_pairs={{16,30},{17,31},{18,28},{19,29},{20,26},{21,27},{22,24},{23,25}} | collective-permute-start | bytes 860168 | tf_op jit(solution)/shard_map/ppermute | solution.py:30
  114.4 52.2 %collective-permute-start.57 = (bf16[160,896]{1,0:T(8,128)(2,1)S(1)}, bf16[160,896]{1,0:T(8,128)(2,1)S(1)}, u32[]{:S(2)}, u32[]{:S(2)}) collective-permute-start(bf16[160,896]{1,0:T(8,128)(2,1)S(1)} %collective-permute-done.56), channel_id=1, source_target_pairs={{4,2},{5,3},{12,10},{13,11},{20,18},{21,19},{28,26},{29,27}} | collective-permute-start | bytes 860168 | tf_op jit(solution)/shard_map/ppermute | solution.py:157
  122.8 44.4 %collective-permute-start.58 = (bf16[160,896]{1,0:T(8,128)(2,1)S(1)}, bf16[160,896]{1,0:T(8,128)(2,1)S(1)}, u32[]{:S(2)}, u32[]{:S(2)}) collective-permute-start(bf16[160,896]{1,0:T(8,128)(2,1)S(1)} %collective-permute-done.56), channel_id=1, source_target_pairs={{4,0},{5,1},{12,8},{13,9},{20,16},{21,17},{28,24},{29,25}} | collective-permute-start | bytes 860168 | tf_op jit(solution)/shard_map/ppermute | solution.py:157
  138.8 16.9 %collective-permute-start.26 = (f32[1,160]{1,0:T(1,128)S(1)}, f32[1,160]{1,0:T(1,128)S(1)}, u32[]{:S(2)}, u32[]{:S(2)}) collective-permute-start(f32[1,160]{1,0:T(1,128)S(1)} %add.431), channel_id=1, source_target_pairs={{0,4},{1,5},{2,6},{3,7},{4,0},{5,1},{6,2},{7,3},{8,12},{9,13},{10,... | collective-permute-start | bytes 1928 | tf_op jit(solution)/shard_map/ppermute | solution.py:30
  145.7 10.7 %collective-permute-start.27 = (f32[1,160]{1,0:T(1,128)S(1)}, f32[1,160]{1,0:T(1,128)S(1)}, u32[]{:S(2)}, u32[]{:S(2)}) collective-permute-start(f32[1,160]{1,0:T(1,128)S(1)} %add.431), channel_id=1, source_target_pairs={{0,6},{1,7},{2,4},{3,5},{4,2},{5,3},{6,0},{7,1},{8,14},{9,15},{10,... | collective-permute-start | bytes 1928 | tf_op jit(solution)/shard_map/ppermute | solution.py:30
  155.8 12.2 %collective-permute-start.59 = (bf16[160,896]{1,0:T(8,128)(2,1)S(1)}, bf16[160,896]{1,0:T(8,128)(2,1)S(1)}, u32[]{:S(2)}, u32[]{:S(2)}) collective-permute-start(bf16[160,896]{1,0:T(8,128)(2,1)S(1)} %collective-permute-done.56), channel_id=1, source_target_pairs={{4,6},{5,7},{12,14},{13,15},{20,22},{21,23},{28,30},{29,31}} | collective-permute-start | bytes 860168 | tf_op jit(solution)/shard_map/ppermute | solution.py:157
  165.1 10.7 %collective-permute-start.30 = (f16[1,160,896]{2,1,0:T(8,128)(2,1)S(1)}, f16[1,160,896]{2,1,0:T(8,128)(2,1)S(1)}, u32[]{:S(2)}, u32[]{:S(2)}) collective-permute-start(f16[1,160,896]{2,1,0:T(8,128)(2,1)S(1)} %fusion.139), channel_id=1, source_target_pairs={{24,16},{25,17},{26,18},{27,19},{28,20},{29,21},{30,22},{31,23}} | collective-permute-start | bytes 860168 | tf_op jit(solution)/shard_map/ppermute | solution.py:30
  166.6 9.2 %collective-permute-start.32 = (f16[1,160,896]{2,1,0:T(8,128)(2,1)S(1)}, f16[1,160,896]{2,1,0:T(8,128)(2,1)S(1)}, u32[]{:S(2)}, u32[]{:S(2)}) collective-permute-start(f16[1,160,896]{2,1,0:T(8,128)(2,1)S(1)} %fusion.140), channel_id=1, source_target_pairs={{24,8},{25,9},{26,10},{27,11},{28,12},{29,13},{30,14},{31,15}} | collective-permute-start | bytes 860168 | tf_op jit(solution)/shard_map/ppermute | solution.py:30
  167.3 8.5 %collective-permute-start.34 = (f16[1,160,896]{2,1,0:T(8,128)(2,1)S(1)}, f16[1,160,896]{2,1,0:T(8,128)(2,1)S(1)}, u32[]{:S(2)}, u32[]{:S(2)}) collective-permute-start(f16[1,160,896]{2,1,0:T(8,128)(2,1)S(1)} %fusion.141), channel_id=1, source_target_pairs={{24,0},{25,1},{26,2},{27,3},{28,4},{29,5},{30,6},{31,7}} | collective-permute-start | bytes 860168 | tf_op jit(solution)/shard_map/ppermute | solution.py:30
  168.0 8.2 %collective-permute-start.60 = (bf16[1,160,896]{2,1,0:T(8,128)(2,1)S(1)}, bf16[1,160,896]{2,1,0:T(8,128)(2,1)S(1)}, u32[]{:S(2)}, u32[]{:S(2)}) collective-permute-start(bf16[1,160,896]{2,1,0:T(8,128)(2,1)S(1)} %select_bitcast_fusion.1), channel_id=1, source_target_pairs={{0,1},{1,0},{2,3},{3,2},{4,5},{5,4},{6,7},{7,6},{8,9},{9,8},{10,11... | collective-permute-start | bytes 860168 | tf_op jit(solution)/shard_map/ppermute | solution.py:30
  168.6 8.1 %collective-permute-start.61 = (bf16[160,896]{1,0:T(8,128)(2,1)S(1)}, bf16[160,896]{1,0:T(8,128)(2,1)S(1)}, u32[]{:S(2)}, u32[]{:S(2)}) collective-permute-start(bf16[160,896]{1,0:T(8,128)(2,1)S(1)} %multiply_convert_fusion.1), channel_id=1, source_target_pairs={{24,4},{25,5},{26,12},{27,13},{28,20},{29,21},{30,28},{31,29}} | collective-permute-start | bytes 860168 | tf_op jit(solution)/shard_map/ppermute | solution.py:30
  176.1 23.6 %collective-permute-start.37 = (f16[1,40,896]{2,1,0:T(8,128)(2,1)S(1)}, f16[1,40,896]{2,1,0:T(8,128)(2,1)S(1)}, u32[]{:S(2)}, u32[]{:S(2)}) collective-permute-start(f16[1,40,896]{2,1,0:T(8,128)(2,1)S(1)} %get-tuple-element.48), channel_id=1, source_target_pairs={{0,2},{1,3},{2,0},{3,1},{4,6},{5,7},{6,4},{7,5},{8,10},{9,11},{10,... | collective-permute-start | bytes 215048 | tf_op jit(solution)/shard_map/ppermute | solution.py:30
  176.7 35.9 %collective-permute-start.62 = (bf16[160,896]{1,0:T(8,128)(2,1)S(1)}, bf16[160,896]{1,0:T(8,128)(2,1)S(1)}, u32[]{:S(2)}, u32[]{:S(2)}) collective-permute-start(bf16[160,896]{1,0:T(8,128)(2,1)S(1)} %collective-permute-done.61), channel_id=1, source_target_pairs={{4,2},{5,3},{12,10},{13,11},{20,18},{21,19},{28,26},{29,27}} | collective-permute-start | bytes 860168 | tf_op jit(solution)/shard_map/ppermute | solution.py:157
  177.4 35.2 %collective-permute-start.63 = (bf16[160,896]{1,0:T(8,128)(2,1)S(1)}, bf16[160,896]{1,0:T(8,128)(2,1)S(1)}, u32[]{:S(2)}, u32[]{:S(2)}) collective-permute-start(bf16[160,896]{1,0:T(8,128)(2,1)S(1)} %collective-permute-done.61), channel_id=1, source_target_pairs={{4,0},{5,1},{12,8},{13,9},{20,16},{21,17},{28,24},{29,25}} | collective-permute-start | bytes 860168 | tf_op jit(solution)/shard_map/ppermute | solution.py:157
  178.7 33.9 %collective-permute-start.64 = (bf16[160,896]{1,0:T(8,128)(2,1)S(1)}, bf16[160,896]{1,0:T(8,128)(2,1)S(1)}, u32[]{:S(2)}, u32[]{:S(2)}) collective-permute-start(bf16[160,896]{1,0:T(8,128)(2,1)S(1)} %collective-permute-done.61), channel_id=1, source_target_pairs={{4,6},{5,7},{12,14},{13,15},{20,22},{21,23},{28,30},{29,31}} | collective-permute-start | bytes 860168 | tf_op jit(solution)/shard_map/ppermute | solution.py:157
  179.4 33.0 %collective-permute-start.36 = (f16[1,40,896]{2,1,0:T(8,128)(2,1)S(1)}, f16[1,40,896]{2,1,0:T(8,128)(2,1)S(1)}, u32[]{:S(2)}, u32[]{:S(2)}) collective-permute-start(f16[1,40,896]{2,1,0:T(8,128)(2,1)S(1)} %get-tuple-element.49), channel_id=1, source_target_pairs={{0,4},{1,5},{2,6},{3,7},{4,0},{5,1},{6,2},{7,3},{8,12},{9,13},{10,... | collective-permute-start | bytes 215048 | tf_op jit(solution)/shard_map/ppermute | solution.py:30
  199.7 12.7 %collective-permute-start.35 = (f16[1,40,896]{2,1,0:T(8,128)(2,1)S(1)}, f16[1,40,896]{2,1,0:T(8,128)(2,1)S(1)}, u32[]{:S(2)}, u32[]{:S(2)}) collective-permute-start(f16[1,40,896]{2,1,0:T(8,128)(2,1)S(1)} %get-tuple-element.47), channel_id=1, source_target_pairs={{0,6},{1,7},{2,4},{3,5},{4,2},{5,3},{6,0},{7,1},{8,14},{9,15},{10,... | collective-permute-start | bytes 215048 | tf_op jit(solution)/shard_map/ppermute | solution.py:30
  212.6 6.4 %collective-permute-start.38 = (bf16[1,40,896]{2,1,0:T(8,128)(2,1)S(1)}, bf16[1,40,896]{2,1,0:T(8,128)(2,1)S(1)}, u32[]{:S(2)}, u32[]{:S(2)}) collective-permute-start(bf16[1,40,896]{2,1,0:T(8,128)(2,1)S(1)} %get-tuple-element.34), channel_id=1, source_target_pairs={{0,6},{1,7},{2,4},{3,5},{4,2},{5,3},{6,0},{7,1},{8,14},{9,15},{10,... | collective-permute-start | bytes 215048 | tf_op jit(solution)/shard_map/ppermute | solution.py:30
  212.8 11.2 %collective-permute-start.65 = (bf16[1,160,896]{2,1,0:T(8,128)(2,1)S(1)}, bf16[1,160,896]{2,1,0:T(8,128)(2,1)S(1)}, u32[]{:S(2)}, u32[]{:S(2)}) collective-permute-start(bf16[1,160,896]{2,1,0:T(8,128)(2,1)S(1)} %select_bitcast_fusion), channel_id=1, source_target_pairs={{0,1},{1,0},{2,3},{3,2},{4,5},{5,4},{6,7},{7,6},{8,9},{9,8},{10,11... | collective-permute-start | bytes 860168 | tf_op jit(solution)/shard_map/ppermute | solution.py:30
  215.1 6.9 %collective-permute-start.39 = (bf16[1,40,896]{2,1,0:T(8,128)(2,1)S(1)}, bf16[1,40,896]{2,1,0:T(8,128)(2,1)S(1)}, u32[]{:S(2)}, u32[]{:S(2)}) collective-permute-start(bf16[1,40,896]{2,1,0:T(8,128)(2,1)S(1)} %get-tuple-element.34), channel_id=1, source_target_pairs={{0,4},{1,5},{2,6},{3,7},{4,0},{5,1},{6,2},{7,3},{8,12},{9,13},{10,... | collective-permute-start | bytes 215048 | tf_op jit(solution)/shard_map/ppermute | solution.py:30
  226.6 24.9 %collective-permute-start.68 = (f16[160,1024]{1,0:T(8,128)(2,1)}, f16[160,1024]{1,0:T(8,128)(2,1)S(1)}, u32[]{:S(2)}, u32[]{:S(2)}) collective-permute-start(f16[160,1024]{1,0:T(8,128)(2,1)} %get-tuple-element.42), channel_id=1, source_target_pairs={{0,8},{1,9},{2,10},{3,11},{4,12},{5,13},{6,14},{7,15},{8,0},{9,1},... | collective-permute-start | bytes 983048 | tf_op jit(solution)/shard_map/ppermute | solution.py:30
  226.6 24.9 %collective-permute-start.67 = (f16[160,1024]{1,0:T(8,128)(2,1)}, f16[160,1024]{1,0:T(8,128)(2,1)S(1)}, u32[]{:S(2)}, u32[]{:S(2)}) collective-permute-start(f16[160,1024]{1,0:T(8,128)(2,1)} %get-tuple-element.43), channel_id=1, source_target_pairs={{0,16},{1,17},{2,18},{3,19},{4,20},{5,21},{6,22},{7,23},{8,24},{9,... | collective-permute-start | bytes 983048 | tf_op jit(solution)/shard_map/ppermute | solution.py:30
  227.0 7.2 %collective-permute-start.46 = (f32[40]{0:T(128)S(1)}, f32[40]{0:T(128)S(1)}, u32[]{:S(2)}, u32[]{:S(2)}) collective-permute-start(f32[40]{0:T(128)S(1)} %get-tuple-element.58), channel_id=1, source_target_pairs={{0,24},{1,25},{2,26},{3,27},{4,28},{5,29},{6,30},{7,31},{8,16},{9,... | collective-permute-start | bytes 488 | tf_op jit(solution)/shard_map/ppermute | solution.py:30
  229.6 6.4 %collective-permute-start.50 = (f32[40]{0:T(128)S(1)}, f32[40]{0:T(128)S(1)}, u32[]{:S(2)}, u32[]{:S(2)}) collective-permute-start(f32[40]{0:T(128)S(1)} %get-tuple-element.59), channel_id=1, source_target_pairs={{0,8},{1,9},{2,10},{3,11},{4,12},{5,13},{6,14},{7,15},{8,0},{9,1},... | collective-permute-start | bytes 488 | tf_op jit(solution)/shard_map/ppermute | solution.py:30
  229.6 7.6 %collective-permute-start.48 = (f32[40]{0:T(128)S(1)}, f32[40]{0:T(128)S(1)}, u32[]{:S(2)}, u32[]{:S(2)}) collective-permute-start(f32[40]{0:T(128)S(1)} %get-tuple-element.60), channel_id=1, source_target_pairs={{0,16},{1,17},{2,18},{3,19},{4,20},{5,21},{6,22},{7,23},{8,24},{9,... | collective-permute-start | bytes 488 | tf_op jit(solution)/shard_map/ppermute | solution.py:30
  237.2 4.9 %collective-permute-start.45 = (f16[40,1024]{1,0:T(8,128)(2,1)S(1)}, f16[40,1024]{1,0:T(8,128)(2,1)S(1)}, u32[]{:S(2)}, u32[]{:S(2)}) collective-permute-start(f16[40,1024]{1,0:T(8,128)(2,1)S(1)} %get-tuple-element.44), channel_id=1, source_target_pairs={{0,24},{1,25},{2,26},{3,27},{4,28},{5,29},{6,30},{7,31},{8,16},{9,... | collective-permute-start | bytes 245768 | tf_op jit(solution)/shard_map/ppermute | solution.py:30
  238.3 13.2 %collective-permute-start.66 = (f16[160,1024]{1,0:T(8,128)(2,1)}, f16[160,1024]{1,0:T(8,128)(2,1)}, u32[]{:S(2)}, u32[]{:S(2)}) collective-permute-start(f16[160,1024]{1,0:T(8,128)(2,1)} %get-tuple-element.41), channel_id=1, source_target_pairs={{0,24},{1,25},{2,26},{3,27},{4,28},{5,29},{6,30},{7,31},{8,16},{9,... | collective-permute-start | bytes 983048 | tf_op jit(solution)/shard_map/ppermute | solution.py:30
  243.3 7.5 %collective-permute-start.52 = (f32[3,40]{1,0:T(4,128)S(1)}, f32[3,40]{1,0:T(4,128)S(1)}, u32[]{:S(2)}, u32[]{:S(2)}) collective-permute-start(f32[3,40]{1,0:T(4,128)S(1)} %pad_maximum_fusion.2), channel_id=1, source_target_pairs={{8,24},{9,25},{10,26},{11,27},{12,28},{13,29},{14,30},{15,31}} | collective-permute-start | bytes 1448 | tf_op jit(solution)/shard_map/ppermute | solution.py:30
  244.0 7.5 %collective-permute-start.53 = (f32[3,40]{1,0:T(4,128)S(1)}, f32[3,40]{1,0:T(4,128)S(1)}, u32[]{:S(2)}, u32[]{:S(2)}) collective-permute-start(f32[3,40]{1,0:T(4,128)S(1)} %pad_maximum_fusion.2), channel_id=1, source_target_pairs={{16,24},{17,25},{18,26},{19,27},{20,28},{21,29},{22,30},{23,31}} | collective-permute-start | bytes 1448 | tf_op jit(solution)/shard_map/ppermute | solution.py:30
  253.1 11.1 %collective-permute-start.69 = (f32[3,160]{1,0:T(4,128)S(1)}, f32[3,160]{1,0:T(4,128)S(1)}, u32[]{:S(2)}, u32[]{:S(2)}) collective-permute-start(f32[3,160]{1,0:T(4,128)S(1)} %maximum_select_fusion), channel_id=1, source_target_pairs={{0,1},{1,0},{2,3},{3,2},{4,5},{5,4},{6,7},{7,6},{8,9},{9,8},{10,11... | collective-permute-start | bytes 5768 | tf_op jit(solution)/shard_map/ppermute | solution.py:30
  (39 other events, 541.0 us)
where the time goes:
time: 273 us; the launch traced here: 270 us
  starting transfers between devices  129 us (47%)
  waiting for transfers between devices  88.3 us (32%)
  matrix products  39.5 us (14%)
  other arithmetic  10.6 us (4%)
    ppermute x67, starting transfers between devices, send(): return lax.ppermute(block, BOTH, pairs)  124 us
    ppermute x67, waiting for transfers between devices, send(): return lax.ppermute(block, BOTH, pairs)  88.2 us
    dot_general x16, matrix products, product(): jnp.dot(rows, columns_of(half, i), preferred_element_type=jnp.float32)  35.1 us
  transfers between devices with their start and end apart: 73, of which 23 were waited for; matrix products, arithmetic and copies ran while one was open for 18% of the time, Pallas kernels for 0%

commit v1 on v0

--- a/solution.py
+++ b/solution.py
@@ -105,16 +105,16 @@
     def product(rows, half, i):
         return jnp.dot(rows, columns_of(half, i), preferred_element_type=jnp.float32)
 
-    def paired_partial(rows, i, embed_product, apart=False):
+    def hidden_product(rows, i, apart):
         partial = product(rows, 0, i)
-        if apart:
-            partial = lax.optimization_barrier(partial)
-        partial = partial * scale[:, None] + embed_product * embed_scale[:, None]
+        return lax.optimization_barrier(partial) if apart else partial
+
+    def paired(partial):
         even, odd = partial[:, :width], partial[:, width:]
         mine = jnp.where(core == 0, even, odd)
         theirs = jnp.where(core == 0, odd, even).astype(WIRE)
         got = grid.swap_core(theirs)
-        return (mine + wide(got)).astype(WIRE)
+        return mine + wide(got)
 
     def gathered_gain():
         parts = [out_gain]
@@ -146,7 +146,7 @@
 
     def broadcast_column(block, at):
         holders = range(at * group, (at + 1) * group)
-        out = [jnp.where(chip == holder, block, jnp.zeros_like(block)) for holder in holders]
+        gots = []
         for d in range(1, chips):
             pairs = [
                 (s * grid.shards + z * CORES + c, s * grid.shards + (z ^ d) * CORES + c)
@@ -155,24 +155,41 @@
                 for c in range(CORES)
             ]
             got = lax.ppermute(block, BOTH, pairs)
-            for r, holder in enumerate(holders):
-                out[r] = jnp.where((chip ^ d) == holder, got, out[r])
+            gots.append(got)
+        out = [jnp.where(chip == holder, block, jnp.zeros_like(block)) for holder in holders]
+        for d, got in zip(range(1, chips), gots):
+            out = [jnp.where((chip ^ d) == holder, got, kept) for holder, kept in zip(holders, out)]
         return jnp.stack(out)
 
     partial_logits = []
     gains = None
-    order = [d for pair in zip(reversed(range(chips)), range(chips)) for d in pair][:chips]
-    embed_products = {}
+    order = [d for d in reversed(range(chips)) if d % 2] + [d for d in reversed(range(chips)) if d % 2 == 0]
+    embed_paired = {}
+    first_scale_here = jnp.where(section == 1, scale, 0.0)
     for k in range(1, depth_count):
         received = []
+        from_neighbour = {}
         rows = narrow(hidden * own_hidden_gain)
         for n, d in enumerate(order):
             if k == 1:
-                embed_products[d] = lax.optimization_barrier(product(embed_input, 1, chip ^ d))
-            paired = paired_partial(rows, chip ^ d, embed_products[d], k > 1 and n == 0)
-            received.append(
-                grid.send(paired, lambda s, z, c: ((s + 1) % sections, z ^ d, c), sources=(k,))
-            )
+                embed_product = lax.optimization_barrier(product(embed_input, 1, chip ^ d))
+                partial = hidden_product(rows, chip ^ d, False) * first_scale_here[:, None]
+                block = paired(partial + embed_product * embed_scale[:, None])
+                embed_paired[d] = block
+            else:
+                partial = hidden_product(rows, chip ^ d, n == 0) * scale[:, None]
+                block = paired(partial) + embed_paired[d]
+            if d % 2:
+                from_neighbour[d - 1] = grid.send(
+                    block.astype(WIRE), lambda s, z, c: (s, z ^ 1, c), sources=(k,)
+                )
+            else:
+                block = block + wide(from_neighbour[d])
+                received.append(
+                    grid.send(
+                        block.astype(WIRE), lambda s, z, c: ((s + 1) % sections, z ^ d, c), sources=(k,)
+                    )
+                )
         if k == 1:
             gains = gathered_gain()
             if group == 1:
@@ -192,7 +209,8 @@
         total = wide(narrow(sum(wide(part) for part in received)))
         arrived = section == k + 1
         hidden = jnp.where(arrived, total, hidden)
-        scale = jnp.where(arrived, scale_of(grid.combine(squares(hidden)[None], add)[0]), scale)
+        hidden_squares = squares(hidden)
+        scale = jnp.where(arrived, scale_of(grid.combine(hidden_squares[None], add)[0]), scale)
         apart, apart_scale = lax.optimization_barrier((hidden, scale))
         rows = narrow(apart * apart_scale[:, None] * gain_slice(k, grid.shard * width, width))
         at = sections // 2
@@ -203,16 +221,19 @@
 
     rows = narrow(hidden * own_hidden_gain)
     part = jnp.zeros((group, tokens, width), WIRE)
+    embed_parts = [embed_paired[d] for d in range(chips)]
     for n, e in enumerate(reversed(range(sections))):
         s = last ^ e
         blocks = []
         for r in range(group):
             i = s * group + r
-            embed_product = embed_products[0]
+            embed_part = embed_parts[0]
             for d in range(1, chips):
-                embed_product = jnp.where((chip ^ d) == i, embed_products[d], embed_product)
-            blocks.append(paired_partial(rows, i, embed_product, n + r == 0))
+                embed_part = jnp.where((chip ^ d) == i, embed_parts[d], embed_part)
+            partial = hidden_product(rows, i, n + r == 0) * scale[:, None]
+            blocks.append((paired(partial) + embed_part).astype(WIRE))
         block = jnp.stack(blocks)
+        embed_parts, block = lax.optimization_barrier((embed_parts, block))
         if s != last:
             block = grid.send(block, lambda a, z, c: (s, z, c), sources=(last,))
         part = jnp.where(section == s, block, part)
@@ -231,31 +252,44 @@
     spread = spread.transpose(1, 0, 2, 3).reshape(group, tokens, width)
     pieces = [wide(piece) for piece in both_halves(spread)]
     last_squares = sum(squares(piece) for piece in pieces)
-    last_scale = scale_of(last_squares, section_width)
+    root = jnp.sqrt(last_squares / section_width)
+    root_high = lax.reduce_precision(root, 5, 10)
+    root_low = lax.reduce_precision((root - root_high) * 1024.0, 5, 10)
+
+    def root_scale(high, low):
+        value = high + low / 1024.0
+        return value * value, lax.rsqrt(value * value + EPSILON)
+
+    mean_square, last_scale = root_scale(root_high, root_low)
     columns = gain_slice(last, section_start, section_width)
     logits = head_product([narrow(piece * columns[i * width : (i + 1) * width]) for i, piece in enumerate(pieces)])
 
     def row_part(values, i):
         return lax.dynamic_slice_in_dim(values, i * part_rows, part_rows, 0)
 
-    sent = (logits * last_scale[:, None]).astype(WIRE)
+    lane = lax.broadcasted_iota(jnp.int32, (tokens, 128), 1)
+    extra = jnp.where(lane == 0, root_high[:, None], jnp.where(lane == 1, root_low[:, None], 0.0))
+    sent = jnp.concatenate([logits * last_scale[:, None], extra], axis=1).astype(WIRE)
     own_logits = row_part(logits, section)
-    square_sum = row_part(last_squares, section)
+    square_sum = row_part(mean_square, section)
     gots = []
     for d in reversed(range(1, sections)):
-        got_squares = grid.swap_section(row_part(last_squares, section ^ d), d)
-        got = grid.swap_section(row_part(sent, section ^ d), d)
-        gots.append((got, got_squares))
-    for got, got_squares in gots:
-        own_logits = own_logits + wide(got) / scale_of(got_squares, section_width)[:, None]
-        square_sum = square_sum + got_squares
-    own_logits = own_logits * scale_of(square_sum)[:, None]
+        gots.append(wide(grid.swap_section(row_part(sent, section ^ d), d)))
+    for got in gots:
+        got_square, got_scale = root_scale(got[:, vocab_width], got[:, vocab_width + 1])
+        own_logits = own_logits + got[:, :vocab_width] / got_scale[:, None]
+        square_sum = square_sum + got_square
+    own_logits = own_logits * scale_of(square_sum, sections)[:, None]
 
     early = jnp.stack(partial_logits + [jnp.zeros_like(partial_logits[0])] * (sections - len(partial_logits)))
     sent = early.astype(WIRE)
     rows = pick_index(early, section)
     for d in reversed(range(1, sections)):
-        got = grid.swap_section(pick_index(sent, section ^ d), d)
+        got = grid.send(
+            pick_index(sent, section ^ d),
+            lambda s, z, c: (s ^ d, z, c),
+            sources=[s for s in range(sections) if s ^ d != last],
+        )
         rows = rows + wide(got)
 
     def statistics(values, targets):

time: 273 us -> 267 us (0.978)
  starting transfers between devices: 129 us -> 115 us
  other arithmetic: 10.6 us -> 15.5 us
  matrix products: 39.5 us -> 42.4 us
    ppermute x67 -> x64, waiting for transfers between devices: 88.2 us -> 73.3 us  [send(): return lax.ppermute(block, BOTH, pairs)]
    ppermute x6, waiting for transfers between devices: 0.02 us -> 14.6 us  [broadcast_column(): got = lax.ppermute(block, BOTH, pairs)]
    ppermute x67 -> x64, starting transfers between devices: 124 us -> 110 us  [send(): return lax.ppermute(block, BOTH, pairs)]
    convert_element_type x20, other arithmetic: 1.58 us -> 5.32 us  [the longest x8 3.84 us: per_device(): block.astype(WIRE)]
    dot_general x16, matrix products: 35.1 us -> 38 us  [product(): jnp.dot(rows, columns_of(half, i), preferred_element_type=jnp.float32)]
  transfers between devices with their start and end apart: 73 -> 70, of which waited for: 23 -> 19; matrix products, arithmetic and copies ran while one was open for 18% -> 20% of each run, Pallas kernels for 0% -> 0%
where the time goes in v1:
time: 267 us; the launch traced here: 265 us
  starting transfers between devices  115 us (43%)
  waiting for transfers between devices  87.8 us (33%)
  matrix products  42.4 us (16%)
  other arithmetic  15.5 us (6%)
    ppermute x64, starting transfers between devices, send(): return lax.ppermute(block, BOTH, pairs)  110 us
    ppermute x64, waiting for transfers between devices, send(): return lax.ppermute(block, BOTH, pairs)  73.3 us
    dot_general x16, matrix products, product(): jnp.dot(rows, columns_of(half, i), preferred_element_type=jnp.float32)  38 us
    ppermute x6, waiting for transfers between devices, broadcast_column(): got = lax.ppermute(block, BOTH, pairs)  14.6 us
    ppermute x6, starting transfers between devices, broadcast_column(): got = lax.ppermute(block, BOTH, pairs)  5.64 us
  transfers between devices with their start and end apart: 70, of which 19 were waited for; matrix products, arithmetic and copies ran while one was open for 20% of the time, Pallas kernels for 0%

profile of v1, /device:TPU:5, one launch (start us, length us, event | category | flops | bytes accessed | tf_op | source)
XLA Modules:
  0.0 264.7 jit_solution(5517293961326142707)
XLA Ops:
  4.9 2.8 %fusion.20 = f32[160,1792]{1,0:T(8,128)S(1)} fusion(bf16[1,2,896,7168]{3,2,1,0:T(8,128)(2,1)} %param.11, s32[]{:T(128)S(6)} %select_n.560, f32[896]{0:T(1024)S(1)} %get-tuple-element.111, bf16[164,896]{1,0:T(8,128)(2,1)} %param.9, s32[]{:T(128)S(6)} %select_n.556), kind=kOutput, calls=%fused_computation.20 | convolution fusion | flops 514232320 | bytes 4648456 | tf_op jit(solution)/shard_map/dot_general | solution.py:106
  7.7 3.7 %fusion.26 = f32[160,1792]{1,0:T(8,128)} fusion(bf16[1,2,896,7168]{3,2,1,0:T(8,128)(2,1)} %param.11, s32[]{:T(128)S(6)} %select_n.554, f32[896]{0:T(1024)S(1)} %get-tuple-element.111, bf16[164,896]{1,0:T(8,128)(2,1)S(1)} %copy-done.3, s32[]{:T(128)S(6)} %select_n.556), kind=kOutput, calls=%fused_computation.26 | convolution fusion | flops 514232320 | bytes 4648968 | tf_op jit(solution)/shard_map/dot_general | solution.py:106
  11.4 2.7 %fusion.8 = f32[160,1792]{1,0:T(8,128)S(1)} fusion(bf16[1,2,896,7168]{3,2,1,0:T(8,128)(2,1)} %param.11, s32[]{:T(128)S(6)} %select_n.566, f32[896]{0:T(1024)S(1)} %get-tuple-element.111, bf16[164,896]{1,0:T(8,128)(2,1)S(1)} %copy-done.3, s32[]{:T(128)S(6)} %select_n.556), kind=kOutput, calls=%fused_computation.8 | convolution fusion | flops 514232320 | bytes 4648968 | tf_op jit(solution)/shard_map/dot_general | solution.py:106
  14.2 3.7 %fusion.14 = f32[160,1792]{1,0:T(8,128)} fusion(bf16[1,2,896,7168]{3,2,1,0:T(8,128)(2,1)} %param.11, s32[]{:T(128)S(6)} %select_n.563, f32[896]{0:T(1024)S(1)} %get-tuple-element.111, bf16[164,896]{1,0:T(8,128)(2,1)S(1)} %copy-done.3, s32[]{:T(128)S(6)} %select_n.556), kind=kOutput, calls=%fused_computation.14 | convolution fusion | flops 514232320 | bytes 4648968 | tf_op jit(solution)/shard_map/dot_general | solution.py:106
  17.9 2.4 collective-permute-start.2
  21.6 2.9 %collective-permute-done.3 = f32[2,160]{1,0:T(2,128)S(1)} collective-permute-done((f32[2,160]{1,0:T(2,128)S(1)}, f32[2,160]{1,0:T(2,128)S(1)}, u32[]{:S(2)}, u32[]{:S(2)}) %collective-permute-start.3) | collective-permute-done | bytes 1312 | tf_op jit(solution)/shard_map/ppermute | solution.py:30
  24.6 2.7 %fusion.60 = f32[160,1792]{1,0:T(8,128)S(1)} fusion(bf16[1,2,896,7168]{3,2,1,0:T(8,128)(2,1)} %param.11, s32[]{:T(128)S(6)} %select_n.560, f32[160,1792]{1,0:T(8,128)S(1)} %fusion.20, f32[160]{0:T(256)S(1)} %bitcast.212, f32[160]{0:T(256)S(1)} %broadcast_select_fusion.20, bf16[160,896]{1,0:T(8,128)(2,1)S(1)} %copy-done.1, f32[896]{0:T(1024)S(1)} %get-tuple-element.110), kind=kOutput, calls=%fused_computation.53 | convolution fusion | flops 515092480 | bytes 5796612 | tf_op jit(solution)/shard_map/dot_general | solution.py:106
  27.4 1.8 collective-permute-start.5
  29.2 2.7 %fusion.51 = f32[160,1792]{1,0:T(8,128)S(1)} fusion(bf16[1,2,896,7168]{3,2,1,0:T(8,128)(2,1)} %param.11, s32[]{:T(128)S(6)} %select_n.554, f32[160,1792]{1,0:T(8,128)S(1)} %copy-done.5, f32[160]{0:T(256)S(1)} %bitcast.213, f32[160]{0:T(256)S(1)} %broadcast_select_fusion.20, bf16[160,896]{1,0:T(8,128)(2,1)S(1)} %copy-done.1, f32[896]{0:T(1024)S(1)} %get-tuple-element.110), kind=kOutput, calls=%fused_computation.50 | convolution fusion | flops 515092480 | bytes 5796612 | tf_op jit(solution)/shard_map/dot_general | solution.py:106
  33.9 2.7 %fusion.78 = f32[160,1792]{1,0:T(8,128)S(1)} fusion(bf16[1,2,896,7168]{3,2,1,0:T(8,128)(2,1)} %param.11, s32[]{:T(128)S(6)} %select_n.566, f32[160,1792]{1,0:T(8,128)S(1)} %fusion.8, f32[160]{0:T(256)S(1)} %bitcast.214, f32[160]{0:T(256)S(1)} %broadcast_select_fusion.20, bf16[160,896]{1,0:T(8,128)(2,1)S(1)} %copy-done.1, f32[896]{0:T(1024)S(1)} %get-tuple-element.110), kind=kOutput, calls=%fused_computation.59 | convolution fusion | flops 515092480 | bytes 5796612 | tf_op jit(solution)/shard_map/dot_general | solution.py:106
  37.9 2.7 %fusion.69 = f32[160,1792]{1,0:T(8,128)S(1)} fusion(bf16[1,2,896,7168]{3,2,1,0:T(8,128)(2,1)} %param.11, s32[]{:T(128)S(6)} %select_n.563, f32[160,1792]{1,0:T(8,128)S(1)} %copy-done.4, f32[160]{0:T(256)S(1)} %bitcast.215, f32[160]{0:T(256)S(1)} %broadcast_select_fusion.20, bf16[160,896]{1,0:T(8,128)(2,1)S(1)} %copy-done.1, f32[896]{0:T(1024)S(1)} %get-tuple-element.110), kind=kOutput, calls=%fused_computation.56 | convolution fusion | flops 515092480 | bytes 5796612 | tf_op jit(solution)/shard_map/dot_general | solution.py:106
  45.1 3.0 %collective-permute-start.44 = (bf16[1,7168]{1,0:T(2,128)(2,1)S(1)}, bf16[1,7168]{1,0:T(2,128)(2,1)S(1)}, u32[]{:S(2)}, u32[]{:S(2)}) collective-permute-start(bf16[1,7168]{1,0:T(2,128)(2,1)S(1)} %copy-done.6), channel_id=1, source_target_pairs={{0,8},{1,9},{2,10},{3,11},{4,12},{5,13},{6,14},{7,15},{8,0},{9,1},... | collective-permute-start | bytes 43016 | tf_op jit(solution)/shard_map/ppermute | solution.py:30
  49.6 6.8 %collective-permute-start.51 = (bf16[160,896]{1,0:T(8,128)(2,1)S(1)}, bf16[160,896]{1,0:T(8,128)(2,1)S(1)}, u32[]{:S(2)}, u32[]{:S(2)}) collective-permute-start(bf16[160,896]{1,0:T(8,128)(2,1)S(1)} %copy-done.1), channel_id=1, source_target_pairs={{0,0},{1,1},{2,8},{3,9},{4,16},{5,17},{6,24},{7,25},{8,2},{9,3},{1... | collective-permute-start | bytes 860168 | tf_op jit(solution)/shard_map/ppermute | solution.py:30
  60.7 11.4 %collective-permute-done.51 = bf16[160,896]{1,0:T(8,128)(2,1)S(1)} collective-permute-done((bf16[160,896]{1,0:T(8,128)(2,1)S(1)}, bf16[160,896]{1,0:T(8,128)(2,1)S(1)}, u32[]{:S(2)}, u32[]{:S(2)}) %collective-permute-start.51) | collective-permute-done | bytes 286752 | tf_op jit(solution)/shard_map/ppermute | solution.py:30
  72.1 1.6 collective-permute-start.52
  73.7 6.8 %collective-permute-done.9 = f16[160,896]{1,0:T(8,128)(2,1)S(1)} collective-permute-done((f16[160,896]{1,0:T(8,128)(2,1)S(1)}, f16[160,896]{1,0:T(8,128)(2,1)S(1)}, u32[]{:S(2)}, u32[]{:S(2)}) %collective-permute-start.9) | collective-permute-done | bytes 286752 | tf_op jit(solution)/shard_map/ppermute | solution.py:30
  80.7 2.2 collective-permute-start.12
  83.8 2.3 collective-permute-start.15
  86.4 2.7 %fusion.10 = f32[160,1792]{1,0:T(8,128)S(1)} fusion(bf16[160,896]{1,0:T(8,128)(2,1)S(1)} %multiply_convert_fusion.4, bf16[1,2,896,7168]{3,2,1,0:T(8,128)(2,1)} %param.11, s32[]{:T(128)S(6)} %select_n.566), kind=kOutput, calls=%fused_computation.10 | convolution fusion | flops 513802240 | bytes 4644868 | tf_op jit(solution)/shard_map/dot_general | solution.py:106
  89.2 2.7 %fusion.63 = f32[160,1792]{1,0:T(8,128)S(1)} fusion(bf16[160,896]{1,0:T(8,128)(2,1)S(1)} %multiply_convert_fusion.4, bf16[1,2,896,7168]{3,2,1,0:T(8,128)(2,1)} %param.11, s32[]{:T(128)S(6)} %select_n.560, f32[160]{0:T(256)S(1)} %broadcast_select_fusion.19), kind=kOutput, calls=%fused_computation.54 | convolution fusion | flops 514088960 | bytes 4645508 | tf_op jit(solution)/shard_map/dot_general | solution.py:106
  91.9 2.9 %fusion.54 = f32[160,1792]{1,0:T(8,128)S(1)} fusion(bf16[160,896]{1,0:T(8,128)(2,1)S(1)} %multiply_convert_fusion.4, bf16[1,2,896,7168]{3,2,1,0:T(8,128)(2,1)} %param.11, s32[]{:T(128)S(6)} %select_n.554, f32[160]{0:T(256)S(1)} %broadcast_select_fusion.19), kind=kOutput, calls=%fused_computation.51 | convolution fusion | flops 514088960 | bytes 4645508 | tf_op jit(solution)/shard_map/dot_general | solution.py:106
  94.8 2.9 %fusion.72 = f32[160,1792]{1,0:T(8,128)S(1)} fusion(bf16[160,896]{1,0:T(8,128)(2,1)S(1)} %multiply_convert_fusion.4, bf16[1,2,896,7168]{3,2,1,0:T(8,128)(2,1)} %param.11, s32[]{:T(128)S(6)} %select_n.563, f32[160]{0:T(256)S(1)} %broadcast_select_fusion.19), kind=kOutput, calls=%fused_computation.57 | convolution fusion | flops 514088960 | bytes 4645508 | tf_op jit(solution)/shard_map/dot_general | solution.py:106
  100.4 1.8 collective-permute-start.53
  102.4 2.9 %collective-permute-start.22 = (f16[160,896]{1,0:T(8,128)(2,1)S(1)}, f16[160,896]{1,0:T(8,128)(2,1)S(1)}, u32[]{:S(2)}, u32[]{:S(2)}) collective-permute-start(f16[160,896]{1,0:T(8,128)(2,1)S(1)} %add_convert_fusion.6), channel_id=1, source_target_pairs={{16,18},{17,19},{18,16},{19,17},{20,22},{21,23},{22,20},{23,21}} | collective-permute-start | bytes 860168 | tf_op jit(solution)/shard_map/ppermute | solution.py:30
  105.4 2.4 collective-permute-start.18
  110.6 3.5 %collective-permute-done.22 = f16[160,896]{1,0:T(8,128)(2,1)S(1)} collective-permute-done((f16[160,896]{1,0:T(8,128)(2,1)S(1)}, f16[160,896]{1,0:T(8,128)(2,1)S(1)}, u32[]{:S(2)}, u32[]{:S(2)}) %collective-permute-start.22) | collective-permute-done | bytes 286752 | tf_op jit(solution)/shard_map/ppermute | solution.py:30
  116.3 4.0 %collective-permute-done.18 = f16[160,896]{1,0:T(8,128)(2,1)S(1)} collective-permute-done((f16[160,896]{1,0:T(8,128)(2,1)S(1)}, f16[160,896]{1,0:T(8,128)(2,1)S(1)}, u32[]{:S(2)}, u32[]{:S(2)}) %collective-permute-start.18) | collective-permute-done | bytes 286752 | tf_op jit(solution)/shard_map/ppermute | solution.py:30
  122.4 14.5 %collective-permute-done.55 = bf16[160,896]{1,0:T(8,128)(2,1)S(1)} collective-permute-done((bf16[160,896]{1,0:T(8,128)(2,1)S(1)}, bf16[160,896]{1,0:T(8,128)(2,1)S(1)}, u32[]{:S(2)}, u32[]{:S(2)}) %collective-permute-start.55) | collective-permute-done | bytes 286752 | tf_op jit(solution)/shard_map/ppermute | solution.py:157
  137.0 2.8 %collective-permute-start.57 = (bf16[1,160,896]{2,1,0:T(8,128)(2,1)S(1)}, bf16[1,160,896]{2,1,0:T(8,128)(2,1)S(1)}, u32[]{:S(2)}, u32[]{:S(2)}) collective-permute-start(bf16[1,160,896]{2,1,0:T(8,128)(2,1)S(1)} %select_bitcast_fusion.1), channel_id=1, source_target_pairs={{0,1},{1,0},{2,3},{3,2},{4,5},{5,4},{6,7},{7,6},{8,9},{9,8},{10,11... | collective-permute-start | bytes 860168 | tf_op jit(solution)/shard_map/ppermute | solution.py:30
  141.3 3.8 %collective-permute-start.26 = (f32[1,160]{1,0:T(1,128)S(1)}, f32[1,160]{1,0:T(1,128)S(1)}, u32[]{:S(2)}, u32[]{:S(2)}) collective-permute-start(f32[1,160]{1,0:T(1,128)S(1)} %add.462), channel_id=1, source_target_pairs={{0,4},{1,5},{2,6},{3,7},{4,0},{5,1},{6,2},{7,3},{8,12},{9,13},{10,... | collective-permute-start | bytes 1928 | tf_op jit(solution)/shard_map/ppermute | solution.py:30
  146.2 3.1 %collective-permute-done.27 = f32[1,160]{1,0:T(1,128)S(1)} collective-permute-done((f32[1,160]{1,0:T(1,128)S(1)}, f32[1,160]{1,0:T(1,128)S(1)}, u32[]{:S(2)}, u32[]{:S(2)}) %collective-permute-start.27) | collective-permute-done | bytes 672 | tf_op jit(solution)/shard_map/ppermute | solution.py:30
  151.9 1.8 collective-permute-start.28
  159.6 7.3 %collective-permute-done.32 = f16[1,160,896]{2,1,0:T(8,128)(2,1)S(1)} collective-permute-done((f16[1,160,896]{2,1,0:T(8,128)(2,1)S(1)}, f16[1,160,896]{2,1,0:T(8,128)(2,1)S(1)}, u32[]{:S(2)}, u32[]{:S(2)}) %collective-permute-start.32) | collective-permute-done | bytes 286752 | tf_op jit(solution)/shard_map/ppermute | solution.py:30
  172.2 12.3 %collective-permute-start.36 = (f16[1,40,896]{2,1,0:T(8,128)(2,1)S(1)}, f16[1,40,896]{2,1,0:T(8,128)(2,1)S(1)}, u32[]{:S(2)}, u32[]{:S(2)}) collective-permute-start(f16[1,40,896]{2,1,0:T(8,128)(2,1)S(1)} %get-tuple-element.95), channel_id=1, source_target_pairs={{0,4},{1,5},{2,6},{3,7},{4,0},{5,1},{6,2},{7,3},{8,12},{9,13},{10,... | collective-permute-start | bytes 215048 | tf_op jit(solution)/shard_map/ppermute | solution.py:30
  185.0 12.2 %collective-permute-done.36 = f16[1,40,896]{2,1,0:T(8,128)(2,1)S(1)} collective-permute-done((f16[1,40,896]{2,1,0:T(8,128)(2,1)S(1)}, f16[1,40,896]{2,1,0:T(8,128)(2,1)S(1)}, u32[]{:S(2)}, u32[]{:S(2)}) %collective-permute-start.36) | collective-permute-done | bytes 71712 | tf_op jit(solution)/shard_map/ppermute | solution.py:30
  197.4 2.9 %collective-permute-start.62 = (bf16[1,160,896]{2,1,0:T(8,128)(2,1)S(1)}, bf16[1,160,896]{2,1,0:T(8,128)(2,1)S(1)}, u32[]{:S(2)}, u32[]{:S(2)}) collective-permute-start(bf16[1,160,896]{2,1,0:T(8,128)(2,1)S(1)} %select_bitcast_fusion), channel_id=1, source_target_pairs={{0,1},{1,0},{2,3},{3,2},{4,5},{5,4},{6,7},{7,6},{8,9},{9,8},{10,11... | collective-permute-start | bytes 860168 | tf_op jit(solution)/shard_map/ppermute | solution.py:30
  200.3 2.5 collective-permute-start.39
  204.1 3.1 %collective-permute-done.39 = bf16[1,40,896]{2,1,0:T(8,128)(2,1)S(1)} collective-permute-done((bf16[1,40,896]{2,1,0:T(8,128)(2,1)S(1)}, bf16[1,40,896]{2,1,0:T(8,128)(2,1)S(1)}, u32[]{:S(2)}, u32[]{:S(2)}) %collective-permute-start.39) | collective-permute-done | bytes 71712 | tf_op jit(solution)/shard_map/ppermute | solution.py:30
  207.4 1.7 collective-permute-start.41
  212.4 5.5 %collective-permute-start.47 = (f16[40,1152]{1,0:T(8,128)(2,1)S(1)}, f16[40,1152]{1,0:T(8,128)(2,1)S(1)}, u32[]{:S(2)}, u32[]{:S(2)}) collective-permute-start(f16[40,1152]{1,0:T(8,128)(2,1)S(1)} %get-tuple-element.92), channel_id=1, source_target_pairs={{0,8},{1,9},{2,10},{3,11},{4,12},{5,13},{6,14},{7,15},{8,0},{9,1},... | collective-permute-start | bytes 276488 | tf_op jit(solution)/shard_map/ppermute | solution.py:30
  220.1 5.9 %collective-permute-start.64 = (f16[160,1024]{1,0:T(8,128)(2,1)}, f16[160,1024]{1,0:T(8,128)(2,1)S(1)}, u32[]{:S(2)}, u32[]{:S(2)}) collective-permute-start(f16[160,1024]{1,0:T(8,128)(2,1)} %get-tuple-element.89), channel_id=1, source_target_pairs={{0,16},{1,17},{2,18},{3,19},{4,20},{5,21},{6,22},{7,23},{16,0},{17... | collective-permute-start | bytes 983048 | tf_op jit(solution)/shard_map/ppermute | solution.py:30
  226.1 1.9 collective-permute-start.63
  228.1 3.0 %collective-permute-start.45 = (f16[40,1152]{1,0:T(8,128)(2,1)S(1)}, f16[40,1152]{1,0:T(8,128)(2,1)S(1)}, u32[]{:S(2)}, u32[]{:S(2)}) collective-permute-start(f16[40,1152]{1,0:T(8,128)(2,1)S(1)} %get-tuple-element.90), channel_id=1, source_target_pairs={{0,24},{1,25},{2,26},{3,27},{4,28},{5,29},{6,30},{7,31},{8,16},{9,... | collective-permute-start | bytes 276488 | tf_op jit(solution)/shard_map/ppermute | solution.py:30
  231.3 13.4 %collective-permute-done.46 = f16[40,1152]{1,0:T(8,128)(2,1)S(1)} collective-permute-done((f16[40,1152]{1,0:T(8,128)(2,1)S(1)}, f16[40,1152]{1,0:T(8,128)(2,1)S(1)}, u32[]{:S(2)}, u32[]{:S(2)}) %collective-permute-start.46) | collective-permute-done | bytes 92192 | tf_op jit(solution)/shard_map/ppermute | solution.py:30
  247.1 5.1 %collective-permute-start.50 = (f32[3,40]{1,0:T(4,128)S(1)}, f32[3,40]{1,0:T(4,128)S(1)}, u32[]{:S(2)}, u32[]{:S(2)}) collective-permute-start(f32[3,40]{1,0:T(4,128)S(1)} %pad_maximum_fusion.2), channel_id=1, source_target_pairs={{16,24},{17,25},{18,26},{19,27},{20,28},{21,29},{22,30},{23,31}} | collective-permute-start | bytes 1448 | tf_op jit(solution)/shard_map/ppermute | solution.py:30
  254.6 3.2 %collective-permute-start.66 = (f32[3,160]{1,0:T(4,128)S(1)}, f32[3,160]{1,0:T(4,128)S(1)}, u32[]{:S(2)}, u32[]{:S(2)}) collective-permute-start(f32[3,160]{1,0:T(4,128)S(1)} %maximum_select_fusion), channel_id=1, source_target_pairs={{0,1},{1,0},{2,3},{3,2},{4,5},{5,4},{6,7},{7,6},{8,9},{9,8},{10,11... | collective-permute-start | bytes 5768 | tf_op jit(solution)/shard_map/ppermute | solution.py:30
  258.7 1.8 collective-permute-start.69
  260.5 1.8 collective-permute-start.67
  (234 shorter events, 63.3 us)
Async XLA Ops:
  2.3 15.7 %collective-permute-start = (f32[2,160]{1,0:T(2,128)S(1)}, f32[2,160]{1,0:T(2,128)S(1)}, u32[]{:S(2)}, u32[]{:S(2)}) collective-permute-start(f32[2,160]{1,0:T(2,128)S(1)} %pad_maximum_fusion.1), channel_id=1, source_target_pairs={{0,1},{1,0},{2,3},{3,2},{4,5},{5,4},{6,7},{7,6},{8,9},{9,8},{10,11... | collective-permute-start | bytes 3848 | tf_op jit(solution)/shard_map/ppermute | solution.py:30
  3.0 56.1 %collective-permute-start.42 = (bf16[1,7168]{1,0:T(2,128)(2,1)}, bf16[1,7168]{1,0:T(2,128)(2,1)S(1)}, u32[]{:S(2)}, u32[]{:S(2)}) collective-permute-start(bf16[1,7168]{1,0:T(2,128)(2,1)} %param.14), channel_id=1, source_target_pairs={{0,24},{1,25},{2,26},{3,27},{4,28},{5,29},{6,30},{7,31},{8,16},{9,... | collective-permute-start | bytes 43016 | tf_op jit(solution)/shard_map/ppermute | solution.py:30
  27.4 13.4 %collective-permute-start.5 = (f16[160,896]{1,0:T(8,128)(2,1)S(1)}, f16[160,896]{1,0:T(8,128)(2,1)S(1)}, u32[]{:S(2)}, u32[]{:S(2)}) collective-permute-start(f16[160,896]{1,0:T(8,128)(2,1)S(1)} %select_convert_fusion.10), channel_id=1, source_target_pairs={{0,1},{1,0},{2,3},{3,2},{4,5},{5,4},{6,7},{7,6},{8,9},{9,8},{10,11... | collective-permute-start | bytes 860168 | tf_op jit(solution)/shard_map/ppermute | solution.py:30
  32.8 11.1 %collective-permute-start.4 = (f16[160,896]{1,0:T(8,128)(2,1)}, f16[160,896]{1,0:T(8,128)(2,1)}, u32[]{:S(2)}, u32[]{:S(2)}) collective-permute-start(f16[160,896]{1,0:T(8,128)(2,1)} %select_convert_fusion.11), channel_id=1, source_target_pairs={{0,1},{1,0},{2,3},{3,2},{4,5},{5,4},{6,7},{7,6},{8,9},{9,8},{10,11... | collective-permute-start | bytes 860168 | tf_op jit(solution)/shard_map/ppermute | solution.py:30
  36.7 5.6 %collective-permute-start.7 = (f16[160,896]{1,0:T(8,128)(2,1)S(1)}, f16[160,896]{1,0:T(8,128)(2,1)S(1)}, u32[]{:S(2)}, u32[]{:S(2)}) collective-permute-start(f16[160,896]{1,0:T(8,128)(2,1)S(1)} %select_convert_fusion.8), channel_id=1, source_target_pairs={{0,1},{1,0},{2,3},{3,2},{4,5},{5,4},{6,7},{7,6},{8,9},{9,8},{10,11... | collective-permute-start | bytes 860168 | tf_op jit(solution)/shard_map/ppermute | solution.py:30
  40.6 9.0 %collective-permute-start.6 = (f16[160,896]{1,0:T(8,128)(2,1)S(1)}, f16[160,896]{1,0:T(8,128)(2,1)}, u32[]{:S(2)}, u32[]{:S(2)}) collective-permute-start(f16[160,896]{1,0:T(8,128)(2,1)S(1)} %select_convert_fusion.9), channel_id=1, source_target_pairs={{0,1},{1,0},{2,3},{3,2},{4,5},{5,4},{6,7},{7,6},{8,9},{9,8},{10,11... | collective-permute-start | bytes 860168 | tf_op jit(solution)/shard_map/ppermute | solution.py:30
  42.3 14.1 %collective-permute-start.8 = (f16[160,896]{1,0:T(8,128)(2,1)S(1)}, f16[160,896]{1,0:T(8,128)(2,1)}, u32[]{:S(2)}, u32[]{:S(2)}) collective-permute-start(f16[160,896]{1,0:T(8,128)(2,1)S(1)} %get-tuple-element.79), channel_id=1, source_target_pairs={{8,10},{9,11},{10,8},{11,9},{12,14},{13,15},{14,12},{15,13}} | collective-permute-start | bytes 860168 | tf_op jit(solution)/shard_map/ppermute | solution.py:30
  43.9 16.7 %collective-permute-start.43 = (bf16[1,7168]{1,0:T(2,128)(2,1)S(1)}, bf16[1,7168]{1,0:T(2,128)(2,1)S(1)}, u32[]{:S(2)}, u32[]{:S(2)}) collective-permute-start(bf16[1,7168]{1,0:T(2,128)(2,1)S(1)} %copy-done.6), channel_id=1, source_target_pairs={{0,16},{1,17},{2,18},{3,19},{4,20},{5,21},{6,22},{7,23},{8,24},{9,... | collective-permute-start | bytes 43016 | tf_op jit(solution)/shard_map/ppermute | solution.py:30
  45.1 15.4 %collective-permute-start.44 = (bf16[1,7168]{1,0:T(2,128)(2,1)S(1)}, bf16[1,7168]{1,0:T(2,128)(2,1)S(1)}, u32[]{:S(2)}, u32[]{:S(2)}) collective-permute-start(bf16[1,7168]{1,0:T(2,128)(2,1)S(1)} %copy-done.6), channel_id=1, source_target_pairs={{0,8},{1,9},{2,10},{3,11},{4,12},{5,13},{6,14},{7,15},{8,0},{9,1},... | collective-permute-start | bytes 43016 | tf_op jit(solution)/shard_map/ppermute | solution.py:30
  49.6 22.5 %collective-permute-start.51 = (bf16[160,896]{1,0:T(8,128)(2,1)S(1)}, bf16[160,896]{1,0:T(8,128)(2,1)S(1)}, u32[]{:S(2)}, u32[]{:S(2)}) collective-permute-start(bf16[160,896]{1,0:T(8,128)(2,1)S(1)} %copy-done.1), channel_id=1, source_target_pairs={{0,0},{1,1},{2,8},{3,9},{4,16},{5,17},{6,24},{7,25},{8,2},{9,3},{1... | collective-permute-start | bytes 860168 | tf_op jit(solution)/shard_map/ppermute | solution.py:30
  56.4 17.3 %collective-permute-start.11 = (f16[160,896]{1,0:T(8,128)(2,1)S(1)}, f16[160,896]{1,0:T(8,128)(2,1)S(1)}, u32[]{:S(2)}, u32[]{:S(2)}) collective-permute-start(f16[160,896]{1,0:T(8,128)(2,1)S(1)} %get-tuple-element.81), channel_id=1, source_target_pairs={{8,16},{9,17},{10,18},{11,19},{12,20},{13,21},{14,22},{15,23}} | collective-permute-start | bytes 860168 | tf_op jit(solution)/shard_map/ppermute | solution.py:30
  59.1 21.4 %collective-permute-start.9 = (f16[160,896]{1,0:T(8,128)(2,1)S(1)}, f16[160,896]{1,0:T(8,128)(2,1)S(1)}, u32[]{:S(2)}, u32[]{:S(2)}) collective-permute-start(f16[160,896]{1,0:T(8,128)(2,1)S(1)} %get-tuple-element.77), channel_id=1, source_target_pairs={{8,20},{9,21},{10,22},{11,23},{12,16},{13,17},{14,18},{15,19}} | collective-permute-start | bytes 860168 | tf_op jit(solution)/shard_map/ppermute | solution.py:30
  72.1 33.3 %collective-permute-start.52 = (bf16[1,160,896]{2,1,0:T(8,128)(2,1)S(1)}, bf16[1,160,896]{2,1,0:T(8,128)(2,1)S(1)}, u32[]{:S(2)}, u32[]{:S(2)}) collective-permute-start(bf16[1,160,896]{2,1,0:T(8,128)(2,1)S(1)} %bitcast.211), channel_id=1, source_target_pairs={{0,1},{1,0},{2,3},{3,2},{4,5},{5,4},{6,7},{7,6},{8,9},{9,8},{10,11... | collective-permute-start | bytes 860168 | tf_op jit(solution)/shard_map/ppermute | solution.py:30
  83.8 5.4 %collective-permute-start.14 = (f32[1,160]{1,0:T(1,128)S(1)}, f32[1,160]{1,0:T(1,128)S(1)}, u32[]{:S(2)}, u32[]{:S(2)}) collective-permute-start(f32[1,160]{1,0:T(1,128)S(1)} %add.446), channel_id=1, source_target_pairs={{0,4},{1,5},{2,6},{3,7},{4,0},{5,1},{6,2},{7,3},{8,12},{9,13},{10,... | collective-permute-start | bytes 1928 | tf_op jit(solution)/shard_map/ppermute | solution.py:30
  83.8 5.4 %collective-permute-start.15 = (f32[1,160]{1,0:T(1,128)S(1)}, f32[1,160]{1,0:T(1,128)S(1)}, u32[]{:S(2)}, u32[]{:S(2)}) collective-permute-start(f32[1,160]{1,0:T(1,128)S(1)} %add.446), channel_id=1, source_target_pairs={{0,6},{1,7},{2,4},{3,5},{4,2},{5,3},{6,0},{7,1},{8,14},{9,15},{10,... | collective-permute-start | bytes 1928 | tf_op jit(solution)/shard_map/ppermute | solution.py:30
  99.3 10.0 %collective-permute-start.20 = (f16[160,896]{1,0:T(8,128)(2,1)S(1)}, f16[160,896]{1,0:T(8,128)(2,1)S(1)}, u32[]{:S(2)}, u32[]{:S(2)}) collective-permute-start(f16[160,896]{1,0:T(8,128)(2,1)S(1)} %select_convert_fusion.5), channel_id=1, source_target_pairs={{0,1},{1,0},{2,3},{3,2},{4,5},{5,4},{6,7},{7,6},{8,9},{9,8},{10,11... | collective-permute-start | bytes 860168 | tf_op jit(solution)/shard_map/ppermute | solution.py:30
  100.2 14.8 %collective-permute-start.16 = (f16[160,896]{1,0:T(8,128)(2,1)S(1)}, f16[160,896]{1,0:T(8,128)(2,1)S(1)}, u32[]{:S(2)}, u32[]{:S(2)}) collective-permute-start(f16[160,896]{1,0:T(8,128)(2,1)S(1)} %select_convert_fusion.7), channel_id=1, source_target_pairs={{0,1},{1,0},{2,3},{3,2},{4,5},{5,4},{6,7},{7,6},{8,9},{9,8},{10,11... | collective-permute-start | bytes 860168 | tf_op jit(solution)/shard_map/ppermute | solution.py:30
  100.4 8.0 %collective-permute-start.53 = (bf16[160,896]{1,0:T(8,128)(2,1)S(1)}, bf16[160,896]{1,0:T(8,128)(2,1)S(1)}, u32[]{:S(2)}, u32[]{:S(2)}) collective-permute-start(bf16[160,896]{1,0:T(8,128)(2,1)S(1)} %multiply_convert_fusion.2), channel_id=1, source_target_pairs={{16,4},{17,5},{18,12},{19,13},{20,20},{21,21},{22,28},{23,29}} | collective-permute-start | bytes 860168 | tf_op jit(solution)/shard_map/ppermute | solution.py:30
  102.4 11.8 %collective-permute-start.22 = (f16[160,896]{1,0:T(8,128)(2,1)S(1)}, f16[160,896]{1,0:T(8,128)(2,1)S(1)}, u32[]{:S(2)}, u32[]{:S(2)}) collective-permute-start(f16[160,896]{1,0:T(8,128)(2,1)S(1)} %add_convert_fusion.6), channel_id=1, source_target_pairs={{16,18},{17,19},{18,16},{19,17},{20,22},{21,23},{22,20},{23,21}} | collective-permute-start | bytes 860168 | tf_op jit(solution)/shard_map/ppermute | solution.py:30
  105.4 14.9 %collective-permute-start.18 = (f16[160,896]{1,0:T(8,128)(2,1)S(1)}, f16[160,896]{1,0:T(8,128)(2,1)S(1)}, u32[]{:S(2)}, u32[]{:S(2)}) collective-permute-start(f16[160,896]{1,0:T(8,128)(2,1)S(1)} %add_convert_fusion.8), channel_id=1, source_target_pairs={{16,18},{17,19},{18,16},{19,17},{20,22},{21,23},{22,20},{23,21}} | collective-permute-start | bytes 860168 | tf_op jit(solution)/shard_map/ppermute | solution.py:30
  108.5 13.9 %collective-permute-start.54 = (bf16[160,896]{1,0:T(8,128)(2,1)S(1)}, bf16[160,896]{1,0:T(8,128)(2,1)S(1)}, u32[]{:S(2)}, u32[]{:S(2)}) collective-permute-start(bf16[160,896]{1,0:T(8,128)(2,1)S(1)} %collective-permute-done.53), channel_id=1, source_target_pairs={{4,2},{5,3},{12,10},{13,11},{20,18},{21,19},{28,26},{29,27}} | collective-permute-start | bytes 860168 | tf_op jit(solution)/shard_map/ppermute | solution.py:157
  109.3 27.6 %collective-permute-start.55 = (bf16[160,896]{1,0:T(8,128)(2,1)S(1)}, bf16[160,896]{1,0:T(8,128)(2,1)S(1)}, u32[]{:S(2)}, u32[]{:S(2)}) collective-permute-start(bf16[160,896]{1,0:T(8,128)(2,1)S(1)} %collective-permute-done.53), channel_id=1, source_target_pairs={{4,0},{5,1},{12,8},{13,9},{20,16},{21,17},{28,24},{29,25}} | collective-permute-start | bytes 860168 | tf_op jit(solution)/shard_map/ppermute | solution.py:157
  114.1 22.8 %collective-permute-start.56 = (bf16[160,896]{1,0:T(8,128)(2,1)S(1)}, bf16[160,896]{1,0:T(8,128)(2,1)S(1)}, u32[]{:S(2)}, u32[]{:S(2)}) collective-permute-start(bf16[160,896]{1,0:T(8,128)(2,1)S(1)} %collective-permute-done.53), channel_id=1, source_target_pairs={{4,6},{5,7},{12,14},{13,15},{20,22},{21,23},{28,30},{29,31}} | collective-permute-start | bytes 860168 | tf_op jit(solution)/shard_map/ppermute | solution.py:157
  115.0 24.8 %collective-permute-start.23 = (f16[160,896]{1,0:T(8,128)(2,1)S(1)}, f16[160,896]{1,0:T(8,128)(2,1)S(1)}, u32[]{:S(2)}, u32[]{:S(2)}) collective-permute-start(f16[160,896]{1,0:T(8,128)(2,1)S(1)} %add_convert_fusion.5), channel_id=1, source_target_pairs={{16,24},{17,25},{18,26},{19,27},{20,28},{21,29},{22,30},{23,31}} | collective-permute-start | bytes 860168 | tf_op jit(solution)/shard_map/ppermute | solution.py:30
  120.5 19.4 %collective-permute-start.19 = (f16[160,896]{1,0:T(8,128)(2,1)S(1)}, f16[160,896]{1,0:T(8,128)(2,1)S(1)}, u32[]{:S(2)}, u32[]{:S(2)}) collective-permute-start(f16[160,896]{1,0:T(8,128)(2,1)S(1)} %add_convert_fusion.7), channel_id=1, source_target_pairs={{16,28},{17,29},{18,30},{19,31},{20,24},{21,25},{22,26},{23,27}} | collective-permute-start | bytes 860168 | tf_op jit(solution)/shard_map/ppermute | solution.py:30
  137.0 31.7 %collective-permute-start.57 = (bf16[1,160,896]{2,1,0:T(8,128)(2,1)S(1)}, bf16[1,160,896]{2,1,0:T(8,128)(2,1)S(1)}, u32[]{:S(2)}, u32[]{:S(2)}) collective-permute-start(bf16[1,160,896]{2,1,0:T(8,128)(2,1)S(1)} %select_bitcast_fusion.1), channel_id=1, source_target_pairs={{0,1},{1,0},{2,3},{3,2},{4,5},{5,4},{6,7},{7,6},{8,9},{9,8},{10,11... | collective-permute-start | bytes 860168 | tf_op jit(solution)/shard_map/ppermute | solution.py:30
  141.3 4.9 %collective-permute-start.26 = (f32[1,160]{1,0:T(1,128)S(1)}, f32[1,160]{1,0:T(1,128)S(1)}, u32[]{:S(2)}, u32[]{:S(2)}) collective-permute-start(f32[1,160]{1,0:T(1,128)S(1)} %add.462), channel_id=1, source_target_pairs={{0,4},{1,5},{2,6},{3,7},{4,0},{5,1},{6,2},{7,3},{8,12},{9,13},{10,... | collective-permute-start | bytes 1928 | tf_op jit(solution)/shard_map/ppermute | solution.py:30
  155.0 14.3 %collective-permute-start.58 = (bf16[160,896]{1,0:T(8,128)(2,1)S(1)}, bf16[160,896]{1,0:T(8,128)(2,1)S(1)}, u32[]{:S(2)}, u32[]{:S(2)}) collective-permute-start(bf16[160,896]{1,0:T(8,128)(2,1)S(1)} %multiply_convert_fusion.1), channel_id=1, source_target_pairs={{24,4},{25,5},{26,12},{27,13},{28,20},{29,21},{30,28},{31,29}} | collective-permute-start | bytes 860168 | tf_op jit(solution)/shard_map/ppermute | solution.py:30
  156.6 10.3 %collective-permute-start.32 = (f16[1,160,896]{2,1,0:T(8,128)(2,1)S(1)}, f16[1,160,896]{2,1,0:T(8,128)(2,1)S(1)}, u32[]{:S(2)}, u32[]{:S(2)}) collective-permute-start(f16[1,160,896]{2,1,0:T(8,128)(2,1)S(1)} %fusion.121), channel_id=1, source_target_pairs={{24,16},{25,17},{26,18},{27,19},{28,20},{29,21},{30,22},{31,23}} | collective-permute-start | bytes 860168 | tf_op jit(solution)/shard_map/ppermute | solution.py:30
  157.9 9.0 %collective-permute-start.33 = (f16[1,160,896]{2,1,0:T(8,128)(2,1)S(1)}, f16[1,160,896]{2,1,0:T(8,128)(2,1)S(1)}, u32[]{:S(2)}, u32[]{:S(2)}) collective-permute-start(f16[1,160,896]{2,1,0:T(8,128)(2,1)S(1)} %fusion.120), channel_id=1, source_target_pairs={{24,8},{25,9},{26,10},{27,11},{28,12},{29,13},{30,14},{31,15}} | collective-permute-start | bytes 860168 | tf_op jit(solution)/shard_map/ppermute | solution.py:30
  158.6 8.3 %collective-permute-start.34 = (f16[1,160,896]{2,1,0:T(8,128)(2,1)S(1)}, f16[1,160,896]{2,1,0:T(8,128)(2,1)S(1)}, u32[]{:S(2)}, u32[]{:S(2)}) collective-permute-start(f16[1,160,896]{2,1,0:T(8,128)(2,1)S(1)} %fusion.119), channel_id=1, source_target_pairs={{24,0},{25,1},{26,2},{27,3},{28,4},{29,5},{30,6},{31,7}} | collective-permute-start | bytes 860168 | tf_op jit(solution)/shard_map/ppermute | solution.py:30
  167.2 17.3 %collective-permute-start.37 = (f16[1,40,896]{2,1,0:T(8,128)(2,1)S(1)}, f16[1,40,896]{2,1,0:T(8,128)(2,1)S(1)}, u32[]{:S(2)}, u32[]{:S(2)}) collective-permute-start(f16[1,40,896]{2,1,0:T(8,128)(2,1)S(1)} %get-tuple-element.94), channel_id=1, source_target_pairs={{0,2},{1,3},{2,0},{3,1},{4,6},{5,7},{6,4},{7,5},{8,10},{9,11},{10,... | collective-permute-start | bytes 215048 | tf_op jit(solution)/shard_map/ppermute | solution.py:30
  169.3 28.0 %collective-permute-start.59 = (bf16[160,896]{1,0:T(8,128)(2,1)S(1)}, bf16[160,896]{1,0:T(8,128)(2,1)S(1)}, u32[]{:S(2)}, u32[]{:S(2)}) collective-permute-start(bf16[160,896]{1,0:T(8,128)(2,1)S(1)} %collective-permute-done.58), channel_id=1, source_target_pairs={{4,2},{5,3},{12,10},{13,11},{20,18},{21,19},{28,26},{29,27}} | collective-permute-start | bytes 860168 | tf_op jit(solution)/shard_map/ppermute | solution.py:157
  169.9 27.4 %collective-permute-start.60 = (bf16[160,896]{1,0:T(8,128)(2,1)S(1)}, bf16[160,896]{1,0:T(8,128)(2,1)S(1)}, u32[]{:S(2)}, u32[]{:S(2)}) collective-permute-start(bf16[160,896]{1,0:T(8,128)(2,1)S(1)} %collective-permute-done.58), channel_id=1, source_target_pairs={{4,0},{5,1},{12,8},{13,9},{20,16},{21,17},{28,24},{29,25}} | collective-permute-start | bytes 860168 | tf_op jit(solution)/shard_map/ppermute | solution.py:157
  171.2 26.1 %collective-permute-start.61 = (bf16[160,896]{1,0:T(8,128)(2,1)S(1)}, bf16[160,896]{1,0:T(8,128)(2,1)S(1)}, u32[]{:S(2)}, u32[]{:S(2)}) collective-permute-start(bf16[160,896]{1,0:T(8,128)(2,1)S(1)} %collective-permute-done.58), channel_id=1, source_target_pairs={{4,6},{5,7},{12,14},{13,15},{20,22},{21,23},{28,30},{29,31}} | collective-permute-start | bytes 860168 | tf_op jit(solution)/shard_map/ppermute | solution.py:157
  172.2 25.0 %collective-permute-start.36 = (f16[1,40,896]{2,1,0:T(8,128)(2,1)S(1)}, f16[1,40,896]{2,1,0:T(8,128)(2,1)S(1)}, u32[]{:S(2)}, u32[]{:S(2)}) collective-permute-start(f16[1,40,896]{2,1,0:T(8,128)(2,1)S(1)} %get-tuple-element.95), channel_id=1, source_target_pairs={{0,4},{1,5},{2,6},{3,7},{4,0},{5,1},{6,2},{7,3},{8,12},{9,13},{10,... | collective-permute-start | bytes 215048 | tf_op jit(solution)/shard_map/ppermute | solution.py:30
  184.4 12.7 %collective-permute-start.35 = (f16[1,40,896]{2,1,0:T(8,128)(2,1)S(1)}, f16[1,40,896]{2,1,0:T(8,128)(2,1)S(1)}, u32[]{:S(2)}, u32[]{:S(2)}) collective-permute-start(f16[1,40,896]{2,1,0:T(8,128)(2,1)S(1)} %get-tuple-element.93), channel_id=1, source_target_pairs={{0,6},{1,7},{2,4},{3,5},{4,2},{5,3},{6,0},{7,1},{8,14},{9,15},{10,... | collective-permute-start | bytes 215048 | tf_op jit(solution)/shard_map/ppermute | solution.py:30
  197.2 6.9 %collective-permute-start.38 = (bf16[1,40,896]{2,1,0:T(8,128)(2,1)S(1)}, bf16[1,40,896]{2,1,0:T(8,128)(2,1)S(1)}, u32[]{:S(2)}, u32[]{:S(2)}) collective-permute-start(bf16[1,40,896]{2,1,0:T(8,128)(2,1)S(1)} %get-tuple-element.72), channel_id=1, source_target_pairs={{0,6},{1,7},{2,4},{3,5},{4,2},{5,3},{6,0},{7,1},{8,14},{9,15},{10,... | collective-permute-start | bytes 215048 | tf_op jit(solution)/shard_map/ppermute | solution.py:30
  197.4 11.7 %collective-permute-start.62 = (bf16[1,160,896]{2,1,0:T(8,128)(2,1)S(1)}, bf16[1,160,896]{2,1,0:T(8,128)(2,1)S(1)}, u32[]{:S(2)}, u32[]{:S(2)}) collective-permute-start(bf16[1,160,896]{2,1,0:T(8,128)(2,1)S(1)} %select_bitcast_fusion), channel_id=1, source_target_pairs={{0,1},{1,0},{2,3},{3,2},{4,5},{5,4},{6,7},{7,6},{8,9},{9,8},{10,11... | collective-permute-start | bytes 860168 | tf_op jit(solution)/shard_map/ppermute | solution.py:30
  200.3 6.9 %collective-permute-start.39 = (bf16[1,40,896]{2,1,0:T(8,128)(2,1)S(1)}, bf16[1,40,896]{2,1,0:T(8,128)(2,1)S(1)}, u32[]{:S(2)}, u32[]{:S(2)}) collective-permute-start(bf16[1,40,896]{2,1,0:T(8,128)(2,1)S(1)} %get-tuple-element.72), channel_id=1, source_target_pairs={{0,4},{1,5},{2,6},{3,7},{4,0},{5,1},{6,2},{7,3},{8,12},{9,13},{10,... | collective-permute-start | bytes 215048 | tf_op jit(solution)/shard_map/ppermute | solution.py:30
  212.4 15.7 %collective-permute-start.47 = (f16[40,1152]{1,0:T(8,128)(2,1)S(1)}, f16[40,1152]{1,0:T(8,128)(2,1)S(1)}, u32[]{:S(2)}, u32[]{:S(2)}) collective-permute-start(f16[40,1152]{1,0:T(8,128)(2,1)S(1)} %get-tuple-element.92), channel_id=1, source_target_pairs={{0,8},{1,9},{2,10},{3,11},{4,12},{5,13},{6,14},{7,15},{8,0},{9,1},... | collective-permute-start | bytes 276488 | tf_op jit(solution)/shard_map/ppermute | solution.py:30
  218.9 34.1 %collective-permute-start.65 = (f16[160,1024]{1,0:T(8,128)(2,1)}, f16[160,1024]{1,0:T(8,128)(2,1)S(1)}, u32[]{:S(2)}, u32[]{:S(2)}) collective-permute-start(f16[160,1024]{1,0:T(8,128)(2,1)} %get-tuple-element.88), channel_id=1, source_target_pairs={{0,8},{1,9},{2,10},{3,11},{4,12},{5,13},{6,14},{7,15},{8,0},{9,1},... | collective-permute-start | bytes 983048 | tf_op jit(solution)/shard_map/ppermute | solution.py:30
  220.1 32.8 %collective-permute-start.64 = (f16[160,1024]{1,0:T(8,128)(2,1)}, f16[160,1024]{1,0:T(8,128)(2,1)S(1)}, u32[]{:S(2)}, u32[]{:S(2)}) collective-permute-start(f16[160,1024]{1,0:T(8,128)(2,1)} %get-tuple-element.89), channel_id=1, source_target_pairs={{0,16},{1,17},{2,18},{3,19},{4,20},{5,21},{6,22},{7,23},{16,0},{17... | collective-permute-start | bytes 983048 | tf_op jit(solution)/shard_map/ppermute | solution.py:30
  226.1 26.9 %collective-permute-start.63 = (f16[160,1024]{1,0:T(8,128)(2,1)}, f16[160,1024]{1,0:T(8,128)(2,1)}, u32[]{:S(2)}, u32[]{:S(2)}) collective-permute-start(f16[160,1024]{1,0:T(8,128)(2,1)} %get-tuple-element.87), channel_id=1, source_target_pairs={{8,16},{9,17},{10,18},{11,19},{12,20},{13,21},{14,22},{15,23},{16,... | collective-permute-start | bytes 983048 | tf_op jit(solution)/shard_map/ppermute | solution.py:30
  228.0 16.7 %collective-permute-start.46 = (f16[40,1152]{1,0:T(8,128)(2,1)S(1)}, f16[40,1152]{1,0:T(8,128)(2,1)S(1)}, u32[]{:S(2)}, u32[]{:S(2)}) collective-permute-start(f16[40,1152]{1,0:T(8,128)(2,1)S(1)} %get-tuple-element.91), channel_id=1, source_target_pairs={{0,16},{1,17},{2,18},{3,19},{4,20},{5,21},{6,22},{7,23},{8,24},{9,... | collective-permute-start | bytes 276488 | tf_op jit(solution)/shard_map/ppermute | solution.py:30
  228.1 16.9 %collective-permute-start.45 = (f16[40,1152]{1,0:T(8,128)(2,1)S(1)}, f16[40,1152]{1,0:T(8,128)(2,1)S(1)}, u32[]{:S(2)}, u32[]{:S(2)}) collective-permute-start(f16[40,1152]{1,0:T(8,128)(2,1)S(1)} %get-tuple-element.90), channel_id=1, source_target_pairs={{0,24},{1,25},{2,26},{3,27},{4,28},{5,29},{6,30},{7,31},{8,16},{9,... | collective-permute-start | bytes 276488 | tf_op jit(solution)/shard_map/ppermute | solution.py:30
  246.4 5.9 %collective-permute-start.49 = (f32[3,40]{1,0:T(4,128)S(1)}, f32[3,40]{1,0:T(4,128)S(1)}, u32[]{:S(2)}, u32[]{:S(2)}) collective-permute-start(f32[3,40]{1,0:T(4,128)S(1)} %pad_maximum_fusion.2), channel_id=1, source_target_pairs={{8,24},{9,25},{10,26},{11,27},{12,28},{13,29},{14,30},{15,31}} | collective-permute-start | bytes 1448 | tf_op jit(solution)/shard_map/ppermute | solution.py:30
  247.1 5.9 %collective-permute-start.50 = (f32[3,40]{1,0:T(4,128)S(1)}, f32[3,40]{1,0:T(4,128)S(1)}, u32[]{:S(2)}, u32[]{:S(2)}) collective-permute-start(f32[3,40]{1,0:T(4,128)S(1)} %pad_maximum_fusion.2), channel_id=1, source_target_pairs={{16,24},{17,25},{18,26},{19,27},{20,28},{21,29},{22,30},{23,31}} | collective-permute-start | bytes 1448 | tf_op jit(solution)/shard_map/ppermute | solution.py:30
  (37 other events, 473.1 us)
